TPU v7x, 32 devices: a whole 2x2x4 slice. The times are simulated.
32 devices in a mesh: ens: 2 (over y), tm: 4 (over x, core), space: 4 (over z).
Axes of the slice: x: 2, y: 2, z: 4, core: 2. Of those that a mesh axis runs over, the one named last changes fastest.
Arguments:
- eigvecs: bfloat16 [8, 2, 3, 2048, 256], P(('ens', 'tm'), None, None, 'space'), parts along dimension 0, may hold values from -6 to 6
- links: bfloat16 [8, 3, 2, 3, 3, 2048], P(('ens', 'tm'), None, None, None, None, 'space'), parts along dimension 0, may hold values from -2.5 to 2.5
- momenta: int32 [3, 3], replicated, may hold values from -2 to 2
- perambulators: bfloat16 [8, 2, 256, 256], P(('ens', 'tm')), parts along dimension 0, may hold values from -0.25 to 0.25
Outputs:
- elementals: bfloat16 [8, 256, 3, 2, 256], P(('ens', 'tm'), 'space'), parts along dimension 0
- projected: bfloat16 [8, 4, 256, 3, 2, 256], P(('ens', 'tm'), None, 'space'), parts along dimension 0
There are 2 independent parts, one for each index of `ens`. A program takes and returns all parts, laid end to end along the dimension named above; an argument that names none is the same for every part. Nothing has to cross between parts.
All inputs are finite; a program needn't handle non-finite values.
Results may differ from a plain program's by a relative error of at most 0.025.
Values may be sent and summed in bfloat16 or wider, within the bound.
No kernel may reach another device: no remote copies, remote signals or barrier semaphores. Data moves between devices by JAX's collectives and lax.ppermute only.
A program may use at most 64 MiB of HBM per device.

v0:
```python
import functools
import math

import jax
import jax.numpy as jnp
from jax import lax
from jax.experimental import pallas as pl
from jax.experimental.pallas import tpu as pltpu
from jax.sharding import PartitionSpec as P

LX = 32
LY = 16
PARTS = 4


def shifted_2(shard, axis, by):
    length = lax.axis_size(axis)
    return lax.ppermute(shard, axis, [(i, (i + by) % length) for i in range(length)])


def phase_angle(momentum, first_pos, second_pos, third_pos, depth):
    weights = momentum.astype(jnp.float32)
    return (
        2.0
        * math.pi
        * (
            weights[0] * first_pos / LX
            + weights[1] * second_pos / LY
            + weights[2] * third_pos / depth
        )
    )


def phased_links(links, momenta, tile_index, tile_count):
    site_count = links.shape[-1]
    planes = site_count // (LX * LY)
    site_index = jnp.arange(site_count, dtype=jnp.int32)
    first_pos = (site_index % LX).astype(jnp.float32)
    second_pos = (site_index // LX % LY).astype(jnp.float32)
    third_pos = (tile_index * planes + site_index // (LX * LY)).astype(jnp.float32)
    angle = jnp.stack(
        [phase_angle(momenta[k], first_pos, second_pos, third_pos, planes * tile_count) for k in range(3)]
    )
    cosine = jnp.cos(angle)[:, None, None]
    sine = jnp.sin(angle)[:, None, None]
    link = links.astype(jnp.float32)
    real = cosine * link[:, 0] + sine * link[:, 1]
    imag = cosine * link[:, 1] - sine * link[:, 0]
    return jnp.stack([real, imag], 3).reshape(3 * 18, site_count).T


def left_rows(source_ref, left_ref):
    _, colors, sites, modes = source_ref.shape
    share = sites // PARTS
    shape = (2 * modes, 2 * modes)
    row = lax.broadcasted_iota(jnp.int32, shape, 0)
    column = lax.broadcasted_iota(jnp.int32, shape, 1)
    one = jnp.ones(shape, jnp.float32)
    zero = jnp.zeros(shape, jnp.float32)
    first = jnp.where(row == 2 * column, one, zero)
    first = first - jnp.where(row == 2 * (column - modes) + 1, one, zero)
    second = jnp.where(row == 2 * column + 1, one, zero)
    second = second + jnp.where(row == 2 * (column - modes), one, zero)
    picks = (first.astype(jnp.bfloat16), second.astype(jnp.bfloat16))
    width = colors * share
    for part in range(PARTS):
        pair = jnp.concatenate(
            [
                source_ref[r, :, part * share : (part + 1) * share, :].reshape(width, modes)
                for r in range(2)
            ],
            1,
        )
        for r in range(2):
            turned = lax.dot_general(
                picks[r], pair, (((1,), (1,)), ((), ())), preferred_element_type=jnp.float32
            )
            start = (part * 2 + r) * width
            left_ref[:, start : start + width] = turned.astype(jnp.bfloat16)


def right_row(block, r, a, share):
    part = block // (share // LX)
    return ((part * 2 + r) * 3 + a - part) * share + block * LX


def color_sum(weight, real, imag, a):
    real_sum = None
    imag_sum = None
    for b in range(3):
        w_real, w_imag = weight(a, b, 0), weight(a, b, 1)
        term_real = w_real * real[b] - w_imag * imag[b]
        term_imag = w_real * imag[b] + w_imag * real[b]
        real_sum = term_real if b == 0 else real_sum + term_real
        imag_sum = term_imag if b == 0 else imag_sum + term_imag
    return real_sum, imag_sum


def store_owned(index_ref, total_ref, outs, slot):
    count = len(outs)
    rows = total_ref.shape[0] // count
    for d in range(count):
        owner = (index_ref[0] + d) % count
        block = total_ref[pl.ds(pl.multiple_of(owner * rows, rows), rows), :]
        outs[d][slot] = block.astype(jnp.bfloat16)


def flat_kernel(index_ref, weights_ref, source_ref, *rest, scale):
    outs, left_ref, wide_ref, right_ref, total_ref = rest[:-4], *rest[-4:]
    sites = source_ref.shape[2]
    share = sites // PARTS
    left_rows(source_ref, left_ref)
    for direction in range(2):

        def step(block, _):
            row = pl.multiple_of(block * LX, LX)
            from_row = row
            if direction == 1:
                plane = block // LY * LY
                from_row = pl.multiple_of((plane + (block - plane + 1) % LY) * LX, LX)
            parts = [
                [source_ref[r, b, pl.ds(from_row, LX), :].astype(jnp.float32) for b in range(3)]
                for r in range(2)
            ]
            if direction == 0:
                parts = [[pltpu.roll(v, LX - 1, 0) for v in part] for part in parts]
            weights = weights_ref[pl.ds(row, LX), :]

            def weight(a, b, r, k=direction):
                column = ((k * 3 + a) * 3 + b) * 2 + r
                return weights[:, column : column + 1]

            for a in range(3):
                for r, value in enumerate(color_sum(weight, *parts, a)):
                    start = pl.multiple_of(right_row(block, r, a, share), LX)
                    right_ref[pl.ds(start, LX), :] = value.astype(jnp.bfloat16)
            if direction == 0:
                for column in range(18):
                    value = weight(0, 0, column, 2).astype(jnp.bfloat16)
                    wide_ref[column, pl.ds(row, LX), :] = jnp.broadcast_to(value, (LX, 128))
            return 0

        lax.fori_loop(0, sites // LX, step, 0)
        total_ref[...] = (
            jnp.dot(left_ref[...], right_ref[...], preferred_element_type=jnp.float32) * scale
        )
        store_owned(index_ref, total_ref, outs, direction)


def deep_kernel(index_ref, left_ref, wide_ref, source_ref, *rest, scale):
    outs, buffer_ref, right_ref, total_ref, sems = rest[:-4], *rest[-4:]
    sites = source_ref.shape[2]
    share = sites // PARTS
    width = left_ref.shape[1] // PARTS
    modes = source_ref.shape[3]
    copies = []
    for part in range(PARTS):
        rows = pl.ds(part * share, share)
        copies.append(
            pltpu.make_async_copy(
                source_ref.at[:, :, rows, :], buffer_ref.at[:, :, rows, :], sems.at[part]
            )
        )
        copies[-1].start()
    for part in range(PARTS):
        copies[part].wait()
        for block in range(part * share // LX, (part + 1) * share // LX):
            row = block * LX
            for lane in range(0, modes, 128):
                real, imag = [
                    [buffer_ref[r, b, row : row + LX, lane : lane + 128] for b in range(3)]
                    for r in range(2)
                ]

                def weight(a, b, r):
                    return wide_ref[(a * 3 + b) * 2 + r, row : row + LX, :]

                for a in range(3):
                    for r, value in enumerate(color_sum(weight, real, imag, a)):
                        start = right_row(block, r, a, share)
                        right_ref[start : start + LX, lane : lane + 128] = value
        value = jnp.dot(
            left_ref[:, part * width : (part + 1) * width],
            right_ref[part * width : (part + 1) * width, :],
            preferred_element_type=jnp.float32,
        )
        if part:
            value = total_ref[...] + value
        if part == PARTS - 1:
            value = value * scale
        total_ref[...] = value
    store_owned(index_ref, total_ref, outs, 0)


def contract_flat(index, weights, vectors, count, scale):
    _, colors, sites, modes = vectors.shape
    depth = 2 * colors * sites
    out = jax.ShapeDtypeStruct((2, 2 * modes // count, modes), jnp.bfloat16)
    vmem = pl.BlockSpec(memory_space=pltpu.VMEM)
    return pl.pallas_call(
        functools.partial(flat_kernel, scale=scale),
        out_shape=[out] * count
        + [
            pltpu.VMEM((2 * modes, depth), jnp.bfloat16),
            pltpu.VMEM((18, sites, 128), jnp.bfloat16),
        ],
        in_specs=[pl.BlockSpec(memory_space=pltpu.SMEM), vmem, vmem],
        out_specs=[vmem] * (count + 2),
        scratch_shapes=[
            pltpu.VMEM((depth, modes), jnp.bfloat16),
            pltpu.VMEM((2 * modes, modes), jnp.float32),
        ],
        cost_estimate=pl.CostEstimate(
            flops=12 * modes * depth * modes, transcendentals=0, bytes_accessed=4 * depth * modes
        ),
        compiler_params=pltpu.CompilerParams(vmem_limit_bytes=24 << 20),
        name="contract_xy",
    )(index, weights, vectors)


def contract_deep(index, left, wide, source, count, scale):
    _, colors, sites, modes = source.shape
    depth = 2 * colors * sites
    out = jax.ShapeDtypeStruct((1, 2 * modes // count, modes), jnp.bfloat16)
    vmem = pl.BlockSpec(memory_space=pltpu.VMEM)
    return pl.pallas_call(
        functools.partial(deep_kernel, scale=scale),
        out_shape=[out] * count,
        in_specs=[
            pl.BlockSpec(memory_space=pltpu.SMEM),
            vmem,
            vmem,
            pl.BlockSpec(memory_space=pl.ANY),
        ],
        out_specs=[vmem] * count,
        scratch_shapes=[
            pltpu.VMEM(source.shape, jnp.bfloat16),
            pltpu.VMEM((depth, modes), jnp.bfloat16),
            pltpu.VMEM((2 * modes, modes), jnp.float32),
            pltpu.SemaphoreType.DMA((PARTS,)),
        ],
        cost_estimate=pl.CostEstimate(
            flops=4 * modes * depth * modes, transcendentals=0, bytes_accessed=2 * depth * modes
        ),
        compiler_params=pltpu.CompilerParams(vmem_limit_bytes=24 << 20),
        name="contract_z",
    )(
        index,
        in_vmem(left),
        in_vmem(wide),
        source,
    )


def owned_sum(blocks):
    total = blocks[0].astype(jnp.float32)
    for block in blocks[1:]:
        total = total + block.astype(jnp.float32)
    return total.astype(blocks[0].dtype)


def project_kernel(index_ref, factor_ref, *rest, count):
    pieces, (own_ref, out_ref) = rest[:count], rest[-2:]
    size, rows, modes = pieces[0].shape
    even = lax.broadcasted_iota(jnp.int32, (rows, modes), 0) % 2 == 0
    for by in range(count):
        section = (index_ref[0] + by) % count
        for k in range(size):
            value = pieces[by][k]
            wide = value.astype(jnp.float32)
            turned = jnp.where(even, -pltpu.roll(wide, rows - 1, 0), pltpu.roll(wide, 1, 0))
            result = jnp.dot(value, factor_ref[0], preferred_element_type=jnp.float32)
            result = result + jnp.dot(
                turned.astype(jnp.bfloat16), factor_ref[1], preferred_element_type=jnp.float32
            )
            out_ref[section, :, k, :, :] = result.astype(jnp.bfloat16).reshape(rows // 2, 2, modes)
            if by == 0:
                own_ref[:, k, :, :] = value.reshape(rows // 2, 2, modes)


def in_vmem(value):
    return pltpu.with_memory_space_constraint(value, pltpu.VMEM)


def project(index, factor, pieces, total, first, earlier):
    count = len(pieces)
    size, rows, modes = pieces[0].shape
    vmem = pl.BlockSpec(memory_space=pltpu.VMEM)
    kept = pl.BlockSpec(memory_space=pl.ANY)
    step = first // size
    return pl.pallas_call(
        functools.partial(project_kernel, count=count),
        grid=(1,),
        out_shape=[
            jax.ShapeDtypeStruct((rows // 2, total, 2, modes), jnp.bfloat16),
            jax.ShapeDtypeStruct((count, rows // 2, total, 2, modes), jnp.bfloat16),
        ],
        in_specs=[pl.BlockSpec(memory_space=pltpu.SMEM)]
        + [vmem] * (1 + count)
        + [kept] * len(earlier),
        out_specs=[
            pl.BlockSpec((rows // 2, size, 2, modes), lambda i: (0, step, 0, 0)),
            pl.BlockSpec((count, rows // 2, size, 2, modes), lambda i: (0, 0, step, 0, 0)),
        ],
        input_output_aliases={2 + count + i: i for i in range(len(earlier))},
    )(index, *[in_vmem(v) for v in (factor, *pieces)], *earlier)


def exchange(blocks, axis):
    return [blocks[0]] + [shifted_2(blocks[by], axis, by) for by in range(1, len(blocks))]


def gather(shard, axis):
    return [shard] + [shifted_2(shard, axis, -by) for by in range(1, lax.axis_size(axis))]


def body(eigvecs, links, momenta, perambulators):
    vectors = eigvecs[0]
    _, _, site_count, _ = vectors.shape
    tile_count = lax.axis_size("space")
    tile_index = lax.axis_index("space")
    plane = LX * LY
    forward = shifted_2(vectors[:, :, :plane], "space", -1)
    scale = 1.0 / math.sqrt(6.0 * site_count * tile_count)
    weights = phased_links(links[0], momenta, tile_index, tile_count)
    tile = tile_index.astype(jnp.int32).reshape(1)
    section = lax.axis_index("tm").astype(jnp.int32).reshape(1)
    *flat, left, wide = contract_flat(tile, weights, vectors, tile_count, scale)
    raised = jnp.concatenate([vectors[:, :, plane:], forward], 2)
    flat_parts = exchange(flat, "space")
    deep = contract_deep(tile, left, wide, raised, tile_count, scale)
    flat_parts, _ = lax.optimization_barrier((flat_parts, deep))
    deep_parts = exchange(deep, "space")
    factor = perambulators[0]
    flat_pieces = gather(owned_sum(flat_parts), "tm")
    earlier = project(section, factor, flat_pieces, 3, 0, ())
    deep_sum = owned_sum(deep_parts)
    deep_pieces = gather(deep_sum, "tm")
    own, projected = project(section, factor, deep_pieces, 3, 2, earlier)
    return (own[None], projected[None])


def solution(mesh):
    in_specs = (
        P(("ens", "tm"), None, None, "space", None),
        P(("ens", "tm"), None, None, None, None, "space"),
        P(),
        P(("ens", "tm"), None, None, None),
    )
    out_specs = (
        P(("ens", "tm"), "space", None, None, None),
        P(("ens", "tm"), None, "space", None, None, None),
    )
    return jax.shard_map(body, mesh=mesh, in_specs=in_specs, out_specs=out_specs, check_vma=False)
```

profile of v0, /device:TPU:25, one launch (start us, length us, event | category | flops | bytes accessed | tf_op | source)
XLA Modules:
  0.0 65.5 jit_solution(2786083257101212584)
XLA Ops:
  0.6 0.2 collective-permute-start
  0.9 0.8 %slice_convert_fusion.2 = (f32[1,3]{1,0:T(1,128)S(1)}, f32[1,3]{1,0:T(1,128)S(1)}, f32[1,3]{1,0:T(1,128)S(1)}) fusion(s32[3,3]{1,0:T(4,128)} %param.6), kind=kLoop, calls=%fused_computation.32 | loop fusion | flops 9 | bytes 72 | tf_op jit(solution)/shard_map/convert_element_type | solution.py:22
  1.6 0.7 %fusion.7 = (f32[1,1]{1,0:T(1,128)}, f32[1,1]{1,0:T(1,128)}, f32[1,1]{1,0:T(1,128)}) fusion(f32[1,3]{1,0:T(1,128)S(1)} %get-tuple-element.42), kind=kLoop, calls=%fused_computation.33 | loop fusion | bytes 24 | tf_op jit(solution)/shard_map/slice | solution.py:27
  2.3 1.9 %add_multiply_fusion.2 = f32[1,512]{1,0:T(1,128)S(1)} fusion(f32[]{:T(128)} %bitcast.5, f32[]{:T(128)} %bitcast.4, s32[]{:T(128)} %axis_index.25, f32[]{:T(128)} %bitcast.3), kind=kLoop, calls=%fused_computation.28 | loop fusion | flops 21504 | bytes 2064 | tf_op jit(solution)/shard_map/mul | solution.py:24
  4.2 0.7 %fusion.9 = (f32[1,1]{1,0:T(1,128)}, f32[1,1]{1,0:T(1,128)}, f32[1,1]{1,0:T(1,128)}) fusion(f32[1,3]{1,0:T(1,128)S(1)} %get-tuple-element.43), kind=kLoop, calls=%fused_computation.35 | loop fusion | bytes 24 | tf_op jit(solution)/shard_map/slice | solution.py:27
  4.9 0.7 %fusion.8 = (f32[1,1]{1,0:T(1,128)}, f32[1,1]{1,0:T(1,128)}, f32[1,1]{1,0:T(1,128)}) fusion(f32[1,3]{1,0:T(1,128)S(1)} %get-tuple-element.44), kind=kLoop, calls=%fused_computation.34 | loop fusion | bytes 24 | tf_op jit(solution)/shard_map/slice | solution.py:27
  5.6 3.9 %add_multiply_fusion = (f32[1,512]{1,0:T(1,128)S(1)}, f32[1,512]{1,0:T(1,128)S(1)}) fusion(f32[]{:T(128)} %bitcast.11, f32[]{:T(128)} %bitcast.10, f32[]{:T(128)} %bitcast.9, s32[]{:T(128)} %axis_index.25, f32[]{:T(128)} %bitcast.8, f32[]{:T(128)} %bitcast.7, f32[]{:T(128)} %bitcast.6), kind=kLoop, calls=%fused_computation.26 | loop fusion | flops 26112 | bytes 4124 | tf_op jit(solution)/shard_map/mul | solution.py:24
  9.5 0.1 fusion.1
  9.6 0.9 %bitcast_convert_fusion = f32[3,2,3,3,512]{4,1,3,2,0:T(2,128)S(1)} fusion(bf16[1,3,2,3,3,512]{5,2,4,3,1,0:T(2,128)(2,1)} %param.5), kind=kLoop, calls=%fused_computation.5 | loop fusion | flops 27648 | bytes 165888 | tf_op jit(solution)/shard_map/convert_element_type | solution.py:46
  10.4 0.1 multiply_add_fusion
  10.6 0.1 pad_maximum_fusion
  10.7 0.1 reshape.320
  10.8 0.1 copy.9
  10.9 0.0 copy-start.1
  10.9 1.4 %copy-done.1 = bf16[1,2,3,512,256]{4,3,2,1,0:T(8,128)(2,1)S(1)} copy-done((bf16[1,2,3,512,256]{4,3,2,1,0:T(8,128)(2,1)S(1)}, bf16[1,2,3,512,256]{4,3,2,1,0:T(8,128)(2,1)}, u32[]{:S(2)}) %copy-start.1) | copy-done | bytes 1572888
  12.3 12.6 %contract_xy.1 = (bf16[2,128,256]{2,1,0:T(8,128)(2,1)S(1)}, bf16[2,128,256]{2,1,0:T(8,128)(2,1)S(1)}, bf16[2,128,256]{2,1,0:T(8,128)(2,1)S(1)}, bf16[2,128,256]{...) custom-call(s32[1]{0:T(128)} %bitcast.2.index_ref, f32[512,54]{1,0:T(8,128)S(1)} %bitcast.33, ...), custom_call_target="tpu_custom_call" | custom-call | flops 2415919104 | bytes 3145728 | tf_op jit(solution)/shard_map/contract_xy/pallas_call | solution.py:200
  24.9 3.1 %collective-permute-start.7 = (bf16[2,128,256]{2,1,0:T(8,128)(2,1)S(1)}, bf16[2,128,256]{2,1,0:T(8,128)(2,1)S(1)}, u32[]{:S(2)}, u32[]{:S(2)}) collective-permute-start(bf16[2,128,256]{2,1,0:T(8,128)(2,1)S(1)} %get-tuple-element.27), channel_id=1, source_target_pairs={{0,1},{1,2},{2,3},{3,0},{4,5},{5,6},{6,7},{7,4},{8,9},{9,10},{10,1... | collective-permute-start | bytes 393224 | tf_op jit(solution)/shard_map/ppermute | solution.py:18
  28.0 0.0 collective-permute-start.8
  28.0 0.4 collective-permute-start.9
  28.4 9.6 %collective-permute-done.source_ref = bf16[2,3,512,256]{3,2,1,0:T(8,128)(2,1)S(1)} collective-permute-done((bf16[2,3,512,256]{3,2,1,0:T(8,128)(2,1)}, bf16[2,3,512,256]{3,2,1,0:T(8,128)(2,1)S(1)}, u32[]{:S(2)}, u32[]{:S(2)}) %collective-permute-start) | collective-permute-done | bytes 1572896 | tf_op jit(solution)/shard_map/ppermute | solution.py:18
  38.0 0.0 copy-start
  38.0 3.1 %contract_z.1 = (bf16[1,128,256]{2,1,0:T(8,128)(2,1)S(1)}, bf16[1,128,256]{2,1,0:T(8,128)(2,1)S(1)}, bf16[1,128,256]{2,1,0:T(8,128)(2,1)S(1)}, bf16[1,128,256]{2,1,0:T(8,128)(2,1)S(1)}) custom-call(s32[1]{0:T(128)} %bitcast.2.index_ref, bf16[512,3072]{1,0:T(8,128)(2,1)S(1)} %get-tuple-element.20.left_ref, ...), custom_call_target="tpu_custom_call" | custom-call | flops 805306368 | bytes 1572864 | tf_op jit(solution)/shard_map/contract_z/pallas_call | solution.py:226
  41.1 0.1 collective-permute-start.1
  41.2 0.1 collective-permute-start.2
  41.3 0.5 collective-permute-done.7
  41.8 1.3 %collective-permute-start.3 = (bf16[1,128,256]{2,1,0:T(8,128)(2,1)S(1)}, bf16[1,128,256]{2,1,0:T(8,128)(2,1)S(1)}, u32[]{:S(2)}, u32[]{:S(2)}) collective-permute-start(bf16[1,128,256]{2,1,0:T(8,128)(2,1)S(1)} %get-tuple-element.25), channel_id=1, source_target_pairs={{0,3},{1,0},{2,1},{3,2},{4,7},{5,4},{6,5},{7,6},{8,11},{9,8},{10,9... | collective-permute-start | bytes 196616 | tf_op jit(solution)/shard_map/ppermute | solution.py:18
  43.1 10.0 %collective-permute-done.8 = bf16[2,128,256]{2,1,0:T(8,128)(2,1)S(1)} collective-permute-done((bf16[2,128,256]{2,1,0:T(8,128)(2,1)S(1)}, bf16[2,128,256]{2,1,0:T(8,128)(2,1)S(1)}, u32[]{:S(2)}, u32[]{:S(2)}) %collective-permute-start.8) | collective-permute-done | bytes 131104 | tf_op jit(solution)/shard_map/ppermute | solution.py:18
  53.1 0.0 collective-permute-done.9
  53.1 0.1 add_convert_fusion.rest_0_
  53.1 1.7 %collective-permute-start.12 = (bf16[2,128,256]{2,1,0:T(8,128)(2,1)S(1)}, bf16[2,128,256]{2,1,0:T(8,128)(2,1)S(1)}, u32[]{:S(2)}, u32[]{:S(2)}) collective-permute-start(bf16[2,128,256]{2,1,0:T(8,128)(2,1)S(1)} %add_convert_fusion.rest_0_), channel_id=1, source_target_pairs={{0,4},{4,8},{8,12},{12,0},{1,5},{5,9},{9,13},{13,1},{2,6},{6,10},{... | collective-permute-start | bytes 393224 | tf_op jit(solution)/shard_map/ppermute | solution.py:18
  54.9 0.3 collective-permute-start.11
  55.1 0.0 collective-permute-done.1
  55.1 0.2 collective-permute-start.10
  55.3 0.5 collective-permute-done.2
  55.9 0.0 collective-permute-done.3
  55.9 1.6 %collective-permute-start.6 = (bf16[1,128,256]{2,1,0:T(8,128)(2,1)S(1)}, bf16[1,128,256]{2,1,0:T(8,128)(2,1)S(1)}, u32[]{:S(2)}, u32[]{:S(2)}) collective-permute-start(bf16[1,128,256]{2,1,0:T(8,128)(2,1)S(1)} %add_convert_fusion.1.rest_0_), channel_id=1, source_target_pairs={{0,4},{4,8},{8,12},{12,0},{1,5},{5,9},{9,13},{13,1},{2,6},{6,10},{... | collective-permute-start | bytes 196616 | tf_op jit(solution)/shard_map/ppermute | solution.py:18
  57.5 0.6 collective-permute-start.5
  58.2 0.0 collective-permute-done.12.rest_3_
  58.2 0.7 %collective-permute-start.4 = (bf16[1,128,256]{2,1,0:T(8,128)(2,1)S(1)}, bf16[1,128,256]{2,1,0:T(8,128)(2,1)S(1)}, u32[]{:S(2)}, u32[]{:S(2)}) collective-permute-start(bf16[1,128,256]{2,1,0:T(8,128)(2,1)S(1)} %add_convert_fusion.1.rest_0_), channel_id=1, source_target_pairs={{0,12},{4,0},{8,4},{12,8},{1,13},{5,1},{9,5},{13,9},{2,14},{6,2},{... | collective-permute-start | bytes 196616 | tf_op jit(solution)/shard_map/ppermute | solution.py:18
  58.9 2.1 %collective-permute-done.11.rest_2_ = bf16[2,128,256]{2,1,0:T(8,128)(2,1)S(1)} collective-permute-done((bf16[2,128,256]{2,1,0:T(8,128)(2,1)S(1)}, bf16[2,128,256]{2,1,0:T(8,128)(2,1)S(1)}, u32[]{:S(2)}, u32[]{:S(2)}) %collective-permute-start.11) | collective-permute-done | bytes 131104 | tf_op jit(solution)/shard_map/ppermute | solution.py:18
  61.0 1.6 %collective-permute-done.10.rest_1_ = bf16[2,128,256]{2,1,0:T(8,128)(2,1)S(1)} collective-permute-done((bf16[2,128,256]{2,1,0:T(8,128)(2,1)S(1)}, bf16[2,128,256]{2,1,0:T(8,128)(2,1)S(1)}, u32[]{:S(2)}, u32[]{:S(2)}) %collective-permute-start.10) | collective-permute-done | bytes 131104 | tf_op jit(solution)/shard_map/ppermute | solution.py:18
  62.6 0.0 copy-done
  62.6 1.4 %shard_map.59 = (bf16[64,3,2,256]{3,2,1,0:T(2,128)(2,1)}, bf16[4,64,3,2,256]{4,3,2,1,0:T(2,128)(2,1)}) custom-call(s32[1]{0:T(128)} %bitcast.index_ref, bf16[2,256,256]{2,1,0:T(8,128)(2,1)S(1)} %bitcast.31, bf16[2,128,256]{2,1,0:T(8,128)(2,1)S(1)} %add_convert_fusion.rest_0_, bf16[2,128,256]{2,1,0:T(8,128)(2,1)S(1)} %collective-permute-done.10.rest_1_, ...), custom_call_target="tpu_custom_call" | custom-call | tf_op jit(solution)/shard_map/pallas_call | solution.py:291
  64.0 0.0 collective-permute-done.6.rest_3_
  64.0 0.0 collective-permute-done.5.rest_2_
  64.1 0.4 collective-permute-done.4.rest_1_
  64.5 1.1 %shard_map.60 = (bf16[64,3,2,256]{3,2,1,0:T(2,128)(2,1)}, bf16[4,64,3,2,256]{4,3,2,1,0:T(2,128)(2,1)}) custom-call(s32[1]{0:T(128)} %bitcast.index_ref, bf16[2,256,256]{2,1,0:T(8,128)(2,1)S(1)} %bitcast.32, bf16[1,128,256]{2,1,0:T(8,128)(2,1)S(1)} %add_convert_fusion.1.rest_0_, ...), custom_call_target="tpu_custom_call", output_to_operand_aliasing={{0}: (6, {}), {1}: (7, {})} | custom-call | tf_op jit(solution)/shard_map/pallas_call | solution.py:291
  (1 shorter events, 0.0 us)
Async XLA Ops:
  0.6 37.4 %collective-permute-start = (bf16[2,3,512,256]{3,2,1,0:T(8,128)(2,1)}, bf16[2,3,512,256]{3,2,1,0:T(8,128)(2,1)S(1)}, u32[]{:S(2)}, u32[]{:S(2)}) collective-permute-start(bf16[2,3,512,256]{3,2,1,0:T(8,128)(2,1)} %bitcast.34), channel_id=1, source_target_pairs={{0,3},{1,0},{2,1},{3,2},{4,7},{5,4},{6,5},{7,6},{8,11},{9,8},{10,9... | collective-permute-start | bytes 4718600 | tf_op jit(solution)/shard_map/ppermute | solution.py:18
  10.9 1.4 %copy-start.1 = (bf16[1,2,3,512,256]{4,3,2,1,0:T(8,128)(2,1)S(1)}, bf16[1,2,3,512,256]{4,3,2,1,0:T(8,128)(2,1)}, u32[]{:S(2)}) copy-start(bf16[1,2,3,512,256]{4,3,2,1,0:T(8,128)(2,1)} %param.4) | copy-start | bytes 4718596
  24.9 16.9 %collective-permute-start.7 = (bf16[2,128,256]{2,1,0:T(8,128)(2,1)S(1)}, bf16[2,128,256]{2,1,0:T(8,128)(2,1)S(1)}, u32[]{:S(2)}, u32[]{:S(2)}) collective-permute-start(bf16[2,128,256]{2,1,0:T(8,128)(2,1)S(1)} %get-tuple-element.27), channel_id=1, source_target_pairs={{0,1},{1,2},{2,3},{3,0},{4,5},{5,6},{6,7},{7,4},{8,9},{9,10},{10,1... | collective-permute-start | bytes 393224 | tf_op jit(solution)/shard_map/ppermute | solution.py:18
  28.0 25.0 %collective-permute-start.8 = (bf16[2,128,256]{2,1,0:T(8,128)(2,1)S(1)}, bf16[2,128,256]{2,1,0:T(8,128)(2,1)S(1)}, u32[]{:S(2)}, u32[]{:S(2)}) collective-permute-start(bf16[2,128,256]{2,1,0:T(8,128)(2,1)S(1)} %get-tuple-element.28), channel_id=1, source_target_pairs={{0,2},{1,3},{2,0},{3,1},{4,6},{5,7},{6,4},{7,5},{8,10},{9,11},{10,... | collective-permute-start | bytes 393224 | tf_op jit(solution)/shard_map/ppermute | solution.py:18
  28.0 25.0 %collective-permute-start.9 = (bf16[2,128,256]{2,1,0:T(8,128)(2,1)S(1)}, bf16[2,128,256]{2,1,0:T(8,128)(2,1)S(1)}, u32[]{:S(2)}, u32[]{:S(2)}) collective-permute-start(bf16[2,128,256]{2,1,0:T(8,128)(2,1)S(1)} %get-tuple-element.29), channel_id=1, source_target_pairs={{0,3},{1,0},{2,1},{3,2},{4,7},{5,4},{6,5},{7,6},{8,11},{9,8},{10,9... | collective-permute-start | bytes 393224 | tf_op jit(solution)/shard_map/ppermute | solution.py:18
  38.0 24.6 %copy-start = (bf16[1,2,256,256]{3,2,1,0:T(8,128)(2,1)S(1)}, bf16[1,2,256,256]{3,2,1,0:T(8,128)(2,1)}, u32[]{:S(2)}) copy-start(bf16[1,2,256,256]{3,2,1,0:T(8,128)(2,1)} %param.7) | copy-start | bytes 786436
  41.1 14.0 %collective-permute-start.1 = (bf16[1,128,256]{2,1,0:T(8,128)(2,1)S(1)}, bf16[1,128,256]{2,1,0:T(8,128)(2,1)S(1)}, u32[]{:S(2)}, u32[]{:S(2)}) collective-permute-start(bf16[1,128,256]{2,1,0:T(8,128)(2,1)S(1)} %get-tuple-element.23), channel_id=1, source_target_pairs={{0,1},{1,2},{2,3},{3,0},{4,5},{5,6},{6,7},{7,4},{8,9},{9,10},{10,1... | collective-permute-start | bytes 196616 | tf_op jit(solution)/shard_map/ppermute | solution.py:18
  41.2 14.6 %collective-permute-start.2 = (bf16[1,128,256]{2,1,0:T(8,128)(2,1)S(1)}, bf16[1,128,256]{2,1,0:T(8,128)(2,1)S(1)}, u32[]{:S(2)}, u32[]{:S(2)}) collective-permute-start(bf16[1,128,256]{2,1,0:T(8,128)(2,1)S(1)} %get-tuple-element.24), channel_id=1, source_target_pairs={{0,2},{1,3},{2,0},{3,1},{4,6},{5,7},{6,4},{7,5},{8,10},{9,11},{10,... | collective-permute-start | bytes 196616 | tf_op jit(solution)/shard_map/ppermute | solution.py:18
  41.8 14.0 %collective-permute-start.3 = (bf16[1,128,256]{2,1,0:T(8,128)(2,1)S(1)}, bf16[1,128,256]{2,1,0:T(8,128)(2,1)S(1)}, u32[]{:S(2)}, u32[]{:S(2)}) collective-permute-start(bf16[1,128,256]{2,1,0:T(8,128)(2,1)S(1)} %get-tuple-element.25), channel_id=1, source_target_pairs={{0,3},{1,0},{2,1},{3,2},{4,7},{5,4},{6,5},{7,6},{8,11},{9,8},{10,9... | collective-permute-start | bytes 196616 | tf_op jit(solution)/shard_map/ppermute | solution.py:18
  53.1 5.1 %collective-permute-start.12 = (bf16[2,128,256]{2,1,0:T(8,128)(2,1)S(1)}, bf16[2,128,256]{2,1,0:T(8,128)(2,1)S(1)}, u32[]{:S(2)}, u32[]{:S(2)}) collective-permute-start(bf16[2,128,256]{2,1,0:T(8,128)(2,1)S(1)} %add_convert_fusion.rest_0_), channel_id=1, source_target_pairs={{0,4},{4,8},{8,12},{12,0},{1,5},{5,9},{9,13},{13,1},{2,6},{6,10},{... | collective-permute-start | bytes 393224 | tf_op jit(solution)/shard_map/ppermute | solution.py:18
  54.9 6.2 %collective-permute-start.11 = (bf16[2,128,256]{2,1,0:T(8,128)(2,1)S(1)}, bf16[2,128,256]{2,1,0:T(8,128)(2,1)S(1)}, u32[]{:S(2)}, u32[]{:S(2)}) collective-permute-start(bf16[2,128,256]{2,1,0:T(8,128)(2,1)S(1)} %add_convert_fusion.rest_0_), channel_id=1, source_target_pairs={{0,8},{4,12},{8,0},{12,4},{1,9},{5,13},{9,1},{13,5},{2,10},{6,14},... | collective-permute-start | bytes 393224 | tf_op jit(solution)/shard_map/ppermute | solution.py:18
  55.1 7.5 %collective-permute-start.10 = (bf16[2,128,256]{2,1,0:T(8,128)(2,1)S(1)}, bf16[2,128,256]{2,1,0:T(8,128)(2,1)S(1)}, u32[]{:S(2)}, u32[]{:S(2)}) collective-permute-start(bf16[2,128,256]{2,1,0:T(8,128)(2,1)S(1)} %add_convert_fusion.rest_0_), channel_id=1, source_target_pairs={{0,12},{4,0},{8,4},{12,8},{1,13},{5,1},{9,5},{13,9},{2,14},{6,2},{... | collective-permute-start | bytes 393224 | tf_op jit(solution)/shard_map/ppermute | solution.py:18
  55.9 8.1 %collective-permute-start.6 = (bf16[1,128,256]{2,1,0:T(8,128)(2,1)S(1)}, bf16[1,128,256]{2,1,0:T(8,128)(2,1)S(1)}, u32[]{:S(2)}, u32[]{:S(2)}) collective-permute-start(bf16[1,128,256]{2,1,0:T(8,128)(2,1)S(1)} %add_convert_fusion.1.rest_0_), channel_id=1, source_target_pairs={{0,4},{4,8},{8,12},{12,0},{1,5},{5,9},{9,13},{13,1},{2,6},{6,10},{... | collective-permute-start | bytes 196616 | tf_op jit(solution)/shard_map/ppermute | solution.py:18
  57.5 6.5 %collective-permute-start.5 = (bf16[1,128,256]{2,1,0:T(8,128)(2,1)S(1)}, bf16[1,128,256]{2,1,0:T(8,128)(2,1)S(1)}, u32[]{:S(2)}, u32[]{:S(2)}) collective-permute-start(bf16[1,128,256]{2,1,0:T(8,128)(2,1)S(1)} %add_convert_fusion.1.rest_0_), channel_id=1, source_target_pairs={{0,8},{4,12},{8,0},{12,4},{1,9},{5,13},{9,1},{13,5},{2,10},{6,14},... | collective-permute-start | bytes 196616 | tf_op jit(solution)/shard_map/ppermute | solution.py:18
  58.2 6.3 %collective-permute-start.4 = (bf16[1,128,256]{2,1,0:T(8,128)(2,1)S(1)}, bf16[1,128,256]{2,1,0:T(8,128)(2,1)S(1)}, u32[]{:S(2)}, u32[]{:S(2)}) collective-permute-start(bf16[1,128,256]{2,1,0:T(8,128)(2,1)S(1)} %add_convert_fusion.1.rest_0_), channel_id=1, source_target_pairs={{0,12},{4,0},{8,4},{12,8},{1,13},{5,1},{9,5},{13,9},{2,14},{6,2},{... | collective-permute-start | bytes 196616 | tf_op jit(solution)/shard_map/ppermute | solution.py:18
where the time goes:
time: 65.9 us; the launch traced here: 65.5 us
  waiting for transfers between devices  24.8 us (38%)
  Pallas kernels  18.1 us (27%)
  starting transfers between devices  10.3 us (16%)
  other arithmetic  7.9 us (12%)
  local copies, waits for them, and re-layouts  3.61 us (5%)
  between operations  0.74 us (1%)
    ppermute x13, waiting for transfers between devices, shifted_2(): lax.ppermute(shard, axis, [(i, (i + by) % length) for i in range(length)])  24.8 us
    pallas_call x1, Pallas kernels, contract_flat(): pl.pallas_call(functools.partial(flat_kernel, scale=scale), out_shape=[ou...  12.6 us
    ppermute x13, starting transfers between devices, shifted_2(): lax.ppermute(shard, axis, [(i, (i + by) % length) for i in range(length)])  10.3 us
    mul x2, other arithmetic, phase_angle(): 2.0 * math.pi  5.84 us
    pallas_call x1, Pallas kernels, contract_deep(): pl.pallas_call(functools.partial(deep_kernel, scale=scale), out_shape=[ou...  3.13 us
    pallas_call x2, Pallas kernels, project(): pl.pallas_call(functools.partial(project_kernel, count=count), grid=(1,),...  2.47 us
    slice x3, local copies, waits for them, and re-layouts, phase_angle(): weights[0] * first_pos / LX + weights[1] * second_pos / LY  1.99 us
    unnamed x4, local copies, waits for them, and re-layouts  1.41 us
  transfers between devices with their start and end apart: 13, of which 7 were waited for; matrix products, arithmetic and copies ran while one was open for 15% of the time, Pallas kernels for 26%

commit v1 on v0

--- a/solution.py
+++ b/solution.py
@@ -263,10 +263,11 @@
     pieces, (own_ref, out_ref) = rest[:count], rest[-2:]
     size, rows, modes = pieces[0].shape
     even = lax.broadcasted_iota(jnp.int32, (rows, modes), 0) % 2 == 0
-    for by in range(count):
-        section = (index_ref[0] + by) % count
+    index = index_ref[0]
+    for piece, (flip, by) in enumerate(section_order(count)):
+        section = (index + by + (1 - 2 * (index % 2)) * flip) % count
         for k in range(size):
-            value = pieces[by][k]
+            value = pieces[piece][k]
             wide = value.astype(jnp.float32)
             turned = jnp.where(even, -pltpu.roll(wide, rows - 1, 0), pltpu.roll(wide, 1, 0))
             result = jnp.dot(value, factor_ref[0], preferred_element_type=jnp.float32)
@@ -274,7 +275,7 @@
                 turned.astype(jnp.bfloat16), factor_ref[1], preferred_element_type=jnp.float32
             )
             out_ref[section, :, k, :, :] = result.astype(jnp.bfloat16).reshape(rows // 2, 2, modes)
-            if by == 0:
+            if piece == 0:
                 own_ref[:, k, :, :] = value.reshape(rows // 2, 2, modes)
 
 
@@ -310,8 +311,32 @@
     return [blocks[0]] + [shifted_2(blocks[by], axis, by) for by in range(1, len(blocks))]
 
 
-def gather(shard, axis):
-    return [shard] + [shifted_2(shard, axis, -by) for by in range(1, lax.axis_size(axis))]
+def paired(axis):
+    length = lax.axis_size(axis)
+    return [(i, i ^ 1) for i in range(length)]
+
+
+def section_order(count):
+    if count % 2:
+        return [(0, by) for by in range(count)]
+    return [(flip, by) for flip in range(2) for by in range(0, count, 2)]
+
+
+def gather(shard, axis, direct):
+    length = lax.axis_size(axis)
+    stride = 1 if length % 2 else 2
+    shards = [shard] + [shifted_2(shard, axis, -by) for by in range(stride, length, stride)]
+    if length % 2:
+        return shards
+    if direct:
+        crossed = [
+            lax.ppermute(shard, axis, [(((i ^ 1) + by) % length, i) for i in range(length)])
+            for by in range(stride, length, stride)
+        ]
+    partner = [lax.ppermute(shard, axis, paired(axis))]
+    if direct:
+        return shards + partner + crossed
+    return shards + partner + [lax.ppermute(v, axis, paired(axis)) for v in shards[1:]]
 
 
 def body(eigvecs, links, momenta, perambulators):
@@ -332,10 +357,11 @@
     flat_parts, _ = lax.optimization_barrier((flat_parts, deep))
     deep_parts = exchange(deep, "space")
     factor = perambulators[0]
-    flat_pieces = gather(owned_sum(flat_parts), "tm")
+    flat_sum = owned_sum(flat_parts)
+    flat_pieces = gather(flat_sum, "tm", False)
     earlier = project(section, factor, flat_pieces, 3, 0, ())
     deep_sum = owned_sum(deep_parts)
-    deep_pieces = gather(deep_sum, "tm")
+    deep_pieces = gather(deep_sum, "tm", True)
     own, projected = project(section, factor, deep_pieces, 3, 2, earlier)
     return (own[None], projected[None])
 

time: 65.9 us -> 69 us (1.047)
  the two profiles are of different devices: /device:TPU:25 before, /device:TPU:0 now
where the time goes in v1:
time: 69 us; the launch traced here: 68.7 us
  starting transfers between devices  19.9 us (29%)
  waiting for transfers between devices  18.4 us (27%)
  Pallas kernels  18.2 us (26%)
  other arithmetic  7.9 us (11%)
  local copies, waits for them, and re-layouts  3.61 us (5%)
  between operations  0.75 us (1%)
    ppermute x9, starting transfers between devices, shifted_2(): lax.ppermute(shard, axis, [(i, (i + by) % length) for i in range(length)])  18.7 us
    ppermute x9, waiting for transfers between devices, shifted_2(): lax.ppermute(shard, axis, [(i, (i + by) % length) for i in range(length)])  18.1 us
    pallas_call x1, Pallas kernels, contract_flat(): pl.pallas_call(functools.partial(flat_kernel, scale=scale), out_shape=[ou...  12.6 us
    mul x2, other arithmetic, phase_angle(): 2.0 * math.pi  5.84 us
    pallas_call x1, Pallas kernels, contract_deep(): pl.pallas_call(functools.partial(deep_kernel, scale=scale), out_shape=[ou...  3.12 us
    pallas_call x2, Pallas kernels, project(): pl.pallas_call(functools.partial(project_kernel, count=count), grid=(1,),...  2.47 us
    slice x3, local copies, waits for them, and re-layouts, phase_angle(): weights[0] * first_pos / LX + weights[1] * second_pos / LY  1.99 us
    unnamed x4, local copies, waits for them, and re-layouts  1.41 us
  transfers between devices with their start and end apart: 13, of which 8 were waited for; matrix products, arithmetic and copies ran while one was open for 15% of the time, Pallas kernels for 25%

profile of v1, /device:TPU:0, one launch (start us, length us, event | category | flops | bytes accessed | tf_op | source)
XLA Modules:
  0.0 68.7 jit_solution(9455588884517682240)
XLA Ops:
  0.6 5.1 %collective-permute-start = (bf16[2,3,512,256]{3,2,1,0:T(8,128)(2,1)}, bf16[2,3,512,256]{3,2,1,0:T(8,128)(2,1)S(1)}, u32[]{:S(2)}, u32[]{:S(2)}) collective-permute-start(bf16[2,3,512,256]{3,2,1,0:T(8,128)(2,1)} %bitcast.34), channel_id=1, source_target_pairs={{0,3},{1,0},{2,1},{3,2},{4,7},{5,4},{6,5},{7,6},{8,11},{9,8},{10,9... | collective-permute-start | bytes 4718600 | tf_op jit(solution)/shard_map/ppermute | solution.py:18
  5.8 0.8 %slice_convert_fusion.2 = (f32[1,3]{1,0:T(1,128)S(1)}, f32[1,3]{1,0:T(1,128)S(1)}, f32[1,3]{1,0:T(1,128)S(1)}) fusion(s32[3,3]{1,0:T(4,128)} %param.6), kind=kLoop, calls=%fused_computation.32 | loop fusion | flops 9 | bytes 72 | tf_op jit(solution)/shard_map/convert_element_type | solution.py:22
  6.6 0.7 fusion.7
  7.2 1.9 %add_multiply_fusion.2 = f32[1,512]{1,0:T(1,128)S(1)} fusion(f32[]{:T(128)} %bitcast.5, f32[]{:T(128)} %bitcast.4, s32[]{:T(128)} %axis_index.25, f32[]{:T(128)} %bitcast.3), kind=kLoop, calls=%fused_computation.28 | loop fusion | flops 21504 | bytes 2064 | tf_op jit(solution)/shard_map/mul | solution.py:24
  9.2 0.7 fusion.9
  9.8 0.7 fusion.8
  10.5 3.9 %add_multiply_fusion = (f32[1,512]{1,0:T(1,128)S(1)}, f32[1,512]{1,0:T(1,128)S(1)}) fusion(f32[]{:T(128)} %bitcast.11, f32[]{:T(128)} %bitcast.10, f32[]{:T(128)} %bitcast.9, s32[]{:T(128)} %axis_index.25, f32[]{:T(128)} %bitcast.8, f32[]{:T(128)} %bitcast.7, f32[]{:T(128)} %bitcast.6), kind=kLoop, calls=%fused_computation.26 | loop fusion | flops 26112 | bytes 4124 | tf_op jit(solution)/shard_map/mul | solution.py:24
  14.4 0.1 fusion.1
  14.5 0.9 %bitcast_convert_fusion = f32[3,2,3,3,512]{4,1,3,2,0:T(2,128)S(1)} fusion(bf16[1,3,2,3,3,512]{5,2,4,3,1,0:T(2,128)(2,1)} %param.5), kind=kLoop, calls=%fused_computation.5 | loop fusion | flops 27648 | bytes 165888 | tf_op jit(solution)/shard_map/convert_element_type | solution.py:46
  15.3 0.1 multiply_add_fusion
  15.5 0.1 pad_maximum_fusion
  15.6 0.1 reshape.320
  15.7 0.1 copy.9
  15.8 0.0 copy-start.1
  15.8 1.4 %copy-done.1 = bf16[1,2,3,512,256]{4,3,2,1,0:T(8,128)(2,1)S(1)} copy-done((bf16[1,2,3,512,256]{4,3,2,1,0:T(8,128)(2,1)S(1)}, bf16[1,2,3,512,256]{4,3,2,1,0:T(8,128)(2,1)}, u32[]{:S(2)}) %copy-start.1) | copy-done | bytes 1572888
  17.2 12.6 %contract_xy.1 = (bf16[2,128,256]{2,1,0:T(8,128)(2,1)S(1)}, bf16[2,128,256]{2,1,0:T(8,128)(2,1)S(1)}, bf16[2,128,256]{2,1,0:T(8,128)(2,1)S(1)}, bf16[2,128,256]{...) custom-call(s32[1]{0:T(128)} %bitcast.2.index_ref, f32[512,54]{1,0:T(8,128)S(1)} %bitcast.33, ...), custom_call_target="tpu_custom_call" | custom-call | flops 2415919104 | bytes 3145728 | tf_op jit(solution)/shard_map/contract_xy/pallas_call | solution.py:200
  29.8 0.1 collective-permute-start.7
  29.9 1.0 %collective-permute-start.8 = (bf16[2,128,256]{2,1,0:T(8,128)(2,1)S(1)}, bf16[2,128,256]{2,1,0:T(8,128)(2,1)S(1)}, u32[]{:S(2)}, u32[]{:S(2)}) collective-permute-start(bf16[2,128,256]{2,1,0:T(8,128)(2,1)S(1)} %get-tuple-element.28), channel_id=1, source_target_pairs={{0,2},{1,3},{2,0},{3,1},{4,6},{5,7},{6,4},{7,5},{8,10},{9,11},{10,... | collective-permute-start | bytes 393224 | tf_op jit(solution)/shard_map/ppermute | solution.py:18
  30.9 2.8 %collective-permute-start.9 = (bf16[2,128,256]{2,1,0:T(8,128)(2,1)S(1)}, bf16[2,128,256]{2,1,0:T(8,128)(2,1)S(1)}, u32[]{:S(2)}, u32[]{:S(2)}) collective-permute-start(bf16[2,128,256]{2,1,0:T(8,128)(2,1)S(1)} %get-tuple-element.29), channel_id=1, source_target_pairs={{0,3},{1,0},{2,1},{3,2},{4,7},{5,4},{6,5},{7,6},{8,11},{9,8},{10,9... | collective-permute-start | bytes 393224 | tf_op jit(solution)/shard_map/ppermute | solution.py:18
  33.7 7.2 %collective-permute-done.source_ref = bf16[2,3,512,256]{3,2,1,0:T(8,128)(2,1)S(1)} collective-permute-done((bf16[2,3,512,256]{3,2,1,0:T(8,128)(2,1)}, bf16[2,3,512,256]{3,2,1,0:T(8,128)(2,1)S(1)}, u32[]{:S(2)}, u32[]{:S(2)}) %collective-permute-start) | collective-permute-done | bytes 1572896 | tf_op jit(solution)/shard_map/ppermute | solution.py:18
  40.9 0.0 copy-start
  40.9 3.1 %contract_z.1 = (bf16[1,128,256]{2,1,0:T(8,128)(2,1)S(1)}, bf16[1,128,256]{2,1,0:T(8,128)(2,1)S(1)}, bf16[1,128,256]{2,1,0:T(8,128)(2,1)S(1)}, bf16[1,128,256]{2,1,0:T(8,128)(2,1)S(1)}) custom-call(s32[1]{0:T(128)} %bitcast.2.index_ref, bf16[512,3072]{1,0:T(8,128)(2,1)S(1)} %get-tuple-element.20.left_ref, ...), custom_call_target="tpu_custom_call" | custom-call | flops 805306368 | bytes 1572864 | tf_op jit(solution)/shard_map/contract_z/pallas_call | solution.py:226
  44.0 0.5 collective-permute-done.7
  44.6 4.5 %collective-permute-done.8 = bf16[2,128,256]{2,1,0:T(8,128)(2,1)S(1)} collective-permute-done((bf16[2,128,256]{2,1,0:T(8,128)(2,1)S(1)}, bf16[2,128,256]{2,1,0:T(8,128)(2,1)S(1)}, u32[]{:S(2)}, u32[]{:S(2)}) %collective-permute-start.8) | collective-permute-done | bytes 131104 | tf_op jit(solution)/shard_map/ppermute | solution.py:18
  49.1 0.0 collective-permute-done.9
  49.1 0.1 add_convert_fusion.rest_0_
  49.1 1.6 %collective-permute-start.10 = (bf16[2,128,256]{2,1,0:T(8,128)(2,1)S(1)}, bf16[2,128,256]{2,1,0:T(8,128)(2,1)S(1)}, u32[]{:S(2)}, u32[]{:S(2)}) collective-permute-start(bf16[2,128,256]{2,1,0:T(8,128)(2,1)S(1)} %add_convert_fusion.rest_0_), channel_id=1, source_target_pairs={{0,8},{4,12},{8,0},{12,4},{1,9},{5,13},{9,1},{13,5},{2,10},{6,14},... | collective-permute-start | bytes 393224 | tf_op jit(solution)/shard_map/ppermute | solution.py:18
  50.7 3.2 %collective-permute-start.1 = (bf16[1,128,256]{2,1,0:T(8,128)(2,1)S(1)}, bf16[1,128,256]{2,1,0:T(8,128)(2,1)S(1)}, u32[]{:S(2)}, u32[]{:S(2)}) collective-permute-start(bf16[1,128,256]{2,1,0:T(8,128)(2,1)S(1)} %get-tuple-element.23), channel_id=1, source_target_pairs={{0,1},{1,2},{2,3},{3,0},{4,5},{5,6},{6,7},{7,4},{8,9},{9,10},{10,1... | collective-permute-start | bytes 196616 | tf_op jit(solution)/shard_map/ppermute | solution.py:18
  54.0 3.4 %collective-permute-start.2 = (bf16[1,128,256]{2,1,0:T(8,128)(2,1)S(1)}, bf16[1,128,256]{2,1,0:T(8,128)(2,1)S(1)}, u32[]{:S(2)}, u32[]{:S(2)}) collective-permute-start(bf16[1,128,256]{2,1,0:T(8,128)(2,1)S(1)} %get-tuple-element.24), channel_id=1, source_target_pairs={{0,2},{1,3},{2,0},{3,1},{4,6},{5,7},{6,4},{7,5},{8,10},{9,11},{10,... | collective-permute-start | bytes 196616 | tf_op jit(solution)/shard_map/ppermute | solution.py:18
  57.3 0.0 collective-permute-start.3
  57.3 0.0 collective-permute-start.11
  57.3 0.0 collective-permute-done.10.rest_1_
  57.3 0.5 collective-permute-start.12
  57.9 2.0 %collective-permute-done.1 = bf16[1,128,256]{2,1,0:T(8,128)(2,1)S(1)} collective-permute-done((bf16[1,128,256]{2,1,0:T(8,128)(2,1)S(1)}, bf16[1,128,256]{2,1,0:T(8,128)(2,1)S(1)}, u32[]{:S(2)}, u32[]{:S(2)}) %collective-permute-start.1) | collective-permute-done | bytes 65568 | tf_op jit(solution)/shard_map/ppermute | solution.py:18
  59.8 1.8 %collective-permute-done.2 = bf16[1,128,256]{2,1,0:T(8,128)(2,1)S(1)} collective-permute-done((bf16[1,128,256]{2,1,0:T(8,128)(2,1)S(1)}, bf16[1,128,256]{2,1,0:T(8,128)(2,1)S(1)}, u32[]{:S(2)}, u32[]{:S(2)}) %collective-permute-start.2) | collective-permute-done | bytes 65568 | tf_op jit(solution)/shard_map/ppermute | solution.py:18
  61.7 0.6 collective-permute-done.3
  62.3 0.1 collective-permute-start.6
  62.4 0.6 collective-permute-start.5
  63.0 1.5 %collective-permute-start.4 = (bf16[1,128,256]{2,1,0:T(8,128)(2,1)S(1)}, bf16[1,128,256]{2,1,0:T(8,128)(2,1)S(1)}, u32[]{:S(2)}, u32[]{:S(2)}) collective-permute-start(bf16[1,128,256]{2,1,0:T(8,128)(2,1)S(1)} %add_convert_fusion.1.rest_0_), channel_id=1, source_target_pairs={{0,8},{4,12},{8,0},{12,4},{1,9},{5,13},{9,1},{13,5},{2,10},{6,14},... | collective-permute-start | bytes 196616 | tf_op jit(solution)/shard_map/ppermute | solution.py:18
  64.5 0.0 collective-permute-done.11.rest_2_
  64.5 0.0 collective-permute-done.12.rest_3_
  64.5 0.0 copy-done
  64.5 1.4 %shard_map.59 = (bf16[64,3,2,256]{3,2,1,0:T(2,128)(2,1)}, bf16[4,64,3,2,256]{4,3,2,1,0:T(2,128)(2,1)}) custom-call(s32[1]{0:T(128)} %bitcast.index_ref, bf16[2,256,256]{2,1,0:T(8,128)(2,1)S(1)} %bitcast.31, bf16[2,128,256]{2,1,0:T(8,128)(2,1)S(1)} %add_convert_fusion.rest_0_, bf16[2,128,256]{2,1,0:T(8,128)(2,1)S(1)} %collective-permute-done.10.rest_1_, ...), custom_call_target="tpu_custom_call" | custom-call | tf_op jit(solution)/shard_map/pallas_call | solution.py:292
  65.9 0.3 collective-permute-done.6.rest_3_
  66.3 0.0 collective-permute-done.5.rest_2_
  66.3 1.4 %collective-permute-done.4.rest_1_ = bf16[1,128,256]{2,1,0:T(8,128)(2,1)S(1)} collective-permute-done((bf16[1,128,256]{2,1,0:T(8,128)(2,1)S(1)}, bf16[1,128,256]{2,1,0:T(8,128)(2,1)S(1)}, u32[]{:S(2)}, u32[]{:S(2)}) %collective-permute-start.4) | collective-permute-done | bytes 65568 | tf_op jit(solution)/shard_map/ppermute | solution.py:18
  67.7 1.1 %shard_map.60 = (bf16[64,3,2,256]{3,2,1,0:T(2,128)(2,1)}, bf16[4,64,3,2,256]{4,3,2,1,0:T(2,128)(2,1)}) custom-call(s32[1]{0:T(128)} %bitcast.index_ref, bf16[2,256,256]{2,1,0:T(8,128)(2,1)S(1)} %bitcast.32, bf16[1,128,256]{2,1,0:T(8,128)(2,1)S(1)} %add_convert_fusion.1.rest_0_, ...), custom_call_target="tpu_custom_call", output_to_operand_aliasing={{0}: (6, {}), {1}: (7, {})} | custom-call | tf_op jit(solution)/shard_map/pallas_call | solution.py:292
  (1 shorter events, 0.0 us)
Async XLA Ops:
  0.6 40.3 %collective-permute-start = (bf16[2,3,512,256]{3,2,1,0:T(8,128)(2,1)}, bf16[2,3,512,256]{3,2,1,0:T(8,128)(2,1)S(1)}, u32[]{:S(2)}, u32[]{:S(2)}) collective-permute-start(bf16[2,3,512,256]{3,2,1,0:T(8,128)(2,1)} %bitcast.34), channel_id=1, source_target_pairs={{0,3},{1,0},{2,1},{3,2},{4,7},{5,4},{6,5},{7,6},{8,11},{9,8},{10,9... | collective-permute-start | bytes 4718600 | tf_op jit(solution)/shard_map/ppermute | solution.py:18
  15.8 1.4 %copy-start.1 = (bf16[1,2,3,512,256]{4,3,2,1,0:T(8,128)(2,1)S(1)}, bf16[1,2,3,512,256]{4,3,2,1,0:T(8,128)(2,1)}, u32[]{:S(2)}) copy-start(bf16[1,2,3,512,256]{4,3,2,1,0:T(8,128)(2,1)} %param.4) | copy-start | bytes 4718596
  29.8 14.8 %collective-permute-start.7 = (bf16[2,128,256]{2,1,0:T(8,128)(2,1)S(1)}, bf16[2,128,256]{2,1,0:T(8,128)(2,1)S(1)}, u32[]{:S(2)}, u32[]{:S(2)}) collective-permute-start(bf16[2,128,256]{2,1,0:T(8,128)(2,1)S(1)} %get-tuple-element.27), channel_id=1, source_target_pairs={{0,1},{1,2},{2,3},{3,0},{4,5},{5,6},{6,7},{7,4},{8,9},{9,10},{10,1... | collective-permute-start | bytes 393224 | tf_op jit(solution)/shard_map/ppermute | solution.py:18
  29.9 19.2 %collective-permute-start.8 = (bf16[2,128,256]{2,1,0:T(8,128)(2,1)S(1)}, bf16[2,128,256]{2,1,0:T(8,128)(2,1)S(1)}, u32[]{:S(2)}, u32[]{:S(2)}) collective-permute-start(bf16[2,128,256]{2,1,0:T(8,128)(2,1)S(1)} %get-tuple-element.28), channel_id=1, source_target_pairs={{0,2},{1,3},{2,0},{3,1},{4,6},{5,7},{6,4},{7,5},{8,10},{9,11},{10,... | collective-permute-start | bytes 393224 | tf_op jit(solution)/shard_map/ppermute | solution.py:18
  30.9 18.2 %collective-permute-start.9 = (bf16[2,128,256]{2,1,0:T(8,128)(2,1)S(1)}, bf16[2,128,256]{2,1,0:T(8,128)(2,1)S(1)}, u32[]{:S(2)}, u32[]{:S(2)}) collective-permute-start(bf16[2,128,256]{2,1,0:T(8,128)(2,1)S(1)} %get-tuple-element.29), channel_id=1, source_target_pairs={{0,3},{1,0},{2,1},{3,2},{4,7},{5,4},{6,5},{7,6},{8,11},{9,8},{10,9... | collective-permute-start | bytes 393224 | tf_op jit(solution)/shard_map/ppermute | solution.py:18
  40.9 23.6 %copy-start = (bf16[1,2,256,256]{3,2,1,0:T(8,128)(2,1)S(1)}, bf16[1,2,256,256]{3,2,1,0:T(8,128)(2,1)}, u32[]{:S(2)}) copy-start(bf16[1,2,256,256]{3,2,1,0:T(8,128)(2,1)} %param.7) | copy-start | bytes 786436
  49.1 8.2 %collective-permute-start.10 = (bf16[2,128,256]{2,1,0:T(8,128)(2,1)S(1)}, bf16[2,128,256]{2,1,0:T(8,128)(2,1)S(1)}, u32[]{:S(2)}, u32[]{:S(2)}) collective-permute-start(bf16[2,128,256]{2,1,0:T(8,128)(2,1)S(1)} %add_convert_fusion.rest_0_), channel_id=1, source_target_pairs={{0,8},{4,12},{8,0},{12,4},{1,9},{5,13},{9,1},{13,5},{2,10},{6,14},... | collective-permute-start | bytes 393224 | tf_op jit(solution)/shard_map/ppermute | solution.py:18
  50.7 9.1 %collective-permute-start.1 = (bf16[1,128,256]{2,1,0:T(8,128)(2,1)S(1)}, bf16[1,128,256]{2,1,0:T(8,128)(2,1)S(1)}, u32[]{:S(2)}, u32[]{:S(2)}) collective-permute-start(bf16[1,128,256]{2,1,0:T(8,128)(2,1)S(1)} %get-tuple-element.23), channel_id=1, source_target_pairs={{0,1},{1,2},{2,3},{3,0},{4,5},{5,6},{6,7},{7,4},{8,9},{9,10},{10,1... | collective-permute-start | bytes 196616 | tf_op jit(solution)/shard_map/ppermute | solution.py:18
  54.0 7.7 %collective-permute-start.2 = (bf16[1,128,256]{2,1,0:T(8,128)(2,1)S(1)}, bf16[1,128,256]{2,1,0:T(8,128)(2,1)S(1)}, u32[]{:S(2)}, u32[]{:S(2)}) collective-permute-start(bf16[1,128,256]{2,1,0:T(8,128)(2,1)S(1)} %get-tuple-element.24), channel_id=1, source_target_pairs={{0,2},{1,3},{2,0},{3,1},{4,6},{5,7},{6,4},{7,5},{8,10},{9,11},{10,... | collective-permute-start | bytes 196616 | tf_op jit(solution)/shard_map/ppermute | solution.py:18
  57.3 4.9 %collective-permute-start.3 = (bf16[1,128,256]{2,1,0:T(8,128)(2,1)S(1)}, bf16[1,128,256]{2,1,0:T(8,128)(2,1)S(1)}, u32[]{:S(2)}, u32[]{:S(2)}) collective-permute-start(bf16[1,128,256]{2,1,0:T(8,128)(2,1)S(1)} %get-tuple-element.25), channel_id=1, source_target_pairs={{0,3},{1,0},{2,1},{3,2},{4,7},{5,4},{6,5},{7,6},{8,11},{9,8},{10,9... | collective-permute-start | bytes 196616 | tf_op jit(solution)/shard_map/ppermute | solution.py:18
  57.3 7.2 %collective-permute-start.11 = (bf16[2,128,256]{2,1,0:T(8,128)(2,1)S(1)}, bf16[2,128,256]{2,1,0:T(8,128)(2,1)S(1)}, u32[]{:S(2)}, u32[]{:S(2)}) collective-permute-start(bf16[2,128,256]{2,1,0:T(8,128)(2,1)S(1)} %add_convert_fusion.rest_0_), channel_id=1, source_target_pairs={{0,4},{4,0},{8,12},{12,8},{1,5},{5,1},{9,13},{13,9},{2,6},{6,2},{1... | collective-permute-start | bytes 393224 | tf_op jit(solution)/shard_map/ppermute | solution.py:336
  57.3 7.2 %collective-permute-start.12 = (bf16[2,128,256]{2,1,0:T(8,128)(2,1)S(1)}, bf16[2,128,256]{2,1,0:T(8,128)(2,1)S(1)}, u32[]{:S(2)}, u32[]{:S(2)}) collective-permute-start(bf16[2,128,256]{2,1,0:T(8,128)(2,1)S(1)} %collective-permute-done.10.rest_1_), channel_id=1, source_target_pairs={{0,4},{4,0},{8,12},{12,8},{1,5},{5,1},{9,13},{13,9},{2,6},{6,2},{1... | collective-permute-start | bytes 393224 | tf_op jit(solution)/shard_map/ppermute | solution.py:339
  62.3 4.0 %collective-permute-start.6 = (bf16[1,128,256]{2,1,0:T(8,128)(2,1)S(1)}, bf16[1,128,256]{2,1,0:T(8,128)(2,1)S(1)}, u32[]{:S(2)}, u32[]{:S(2)}) collective-permute-start(bf16[1,128,256]{2,1,0:T(8,128)(2,1)S(1)} %add_convert_fusion.1.rest_0_), channel_id=1, source_target_pairs={{12,0},{8,4},{4,8},{0,12},{13,1},{9,5},{5,9},{1,13},{14,2},{10,6},... | collective-permute-start | bytes 196616 | tf_op jit(solution)/shard_map/ppermute | solution.py:333
  62.4 3.9 %collective-permute-start.5 = (bf16[1,128,256]{2,1,0:T(8,128)(2,1)S(1)}, bf16[1,128,256]{2,1,0:T(8,128)(2,1)S(1)}, u32[]{:S(2)}, u32[]{:S(2)}) collective-permute-start(bf16[1,128,256]{2,1,0:T(8,128)(2,1)S(1)} %add_convert_fusion.1.rest_0_), channel_id=1, source_target_pairs={{0,4},{4,0},{8,12},{12,8},{1,5},{5,1},{9,13},{13,9},{2,6},{6,2},{1... | collective-permute-start | bytes 196616 | tf_op jit(solution)/shard_map/ppermute | solution.py:336
  63.0 4.6 %collective-permute-start.4 = (bf16[1,128,256]{2,1,0:T(8,128)(2,1)S(1)}, bf16[1,128,256]{2,1,0:T(8,128)(2,1)S(1)}, u32[]{:S(2)}, u32[]{:S(2)}) collective-permute-start(bf16[1,128,256]{2,1,0:T(8,128)(2,1)S(1)} %add_convert_fusion.1.rest_0_), channel_id=1, source_target_pairs={{0,8},{4,12},{8,0},{12,4},{1,9},{5,13},{9,1},{13,5},{2,10},{6,14},... | collective-permute-start | bytes 196616 | tf_op jit(solution)/shard_map/ppermute | solution.py:18

commit v2 on v1

--- a/solution.py
+++ b/solution.py
@@ -259,56 +259,77 @@
     return total.astype(blocks[0].dtype)
 
 
-def project_kernel(index_ref, factor_ref, *rest, count):
-    pieces, (own_ref, out_ref) = rest[:count], rest[-2:]
-    size, rows, modes = pieces[0].shape
-    even = lax.broadcasted_iota(jnp.int32, (rows, modes), 0) % 2 == 0
+def in_vmem(value):
+    return pltpu.with_memory_space_constraint(value, pltpu.VMEM)
+
+
+def project_kernel(index_ref, factor_ref, *rest, plan, count, aliased):
+    items = len(plan)
+    pieces, rest = rest[:items], rest[items + aliased :]
+    own_ref, out_ref, sems = rest[0], rest[1], rest[-1]
+    buffers = list(rest[2:-1])
     index = index_ref[0]
-    for piece, (flip, by) in enumerate(section_order(count)):
+    copies = []
+    for slot, (flip, by, first) in enumerate(plan):
+        piece_ref, buffer_ref = pieces[slot], buffers[slot]
+        size, rows, modes = piece_ref.shape
         section = (index + by + (1 - 2 * (index % 2)) * flip) % count
+        even = lax.broadcasted_iota(jnp.int32, (rows, modes), 0) % 2 == 0
         for k in range(size):
-            value = pieces[piece][k]
+            value = piece_ref[k]
             wide = value.astype(jnp.float32)
             turned = jnp.where(even, -pltpu.roll(wide, rows - 1, 0), pltpu.roll(wide, 1, 0))
             result = jnp.dot(value, factor_ref[0], preferred_element_type=jnp.float32)
             result = result + jnp.dot(
                 turned.astype(jnp.bfloat16), factor_ref[1], preferred_element_type=jnp.float32
             )
-            out_ref[section, :, k, :, :] = result.astype(jnp.bfloat16).reshape(rows // 2, 2, modes)
-            if piece == 0:
-                own_ref[:, k, :, :] = value.reshape(rows // 2, 2, modes)
-
-
-def in_vmem(value):
-    return pltpu.with_memory_space_constraint(value, pltpu.VMEM)
-
-
-def project(index, factor, pieces, total, first, earlier):
-    count = len(pieces)
-    size, rows, modes = pieces[0].shape
+            buffer_ref[:, k, :, :] = result.astype(jnp.bfloat16).reshape(rows // 2, 2, modes)
+        momenta = pl.ds(first, size)
+        copies.append(
+            pltpu.make_async_copy(buffer_ref, out_ref.at[section, :, momenta], sems.at[len(copies)])
+        )
+        copies[-1].start()
+        if flip == 0 and by == 0:
+            kept_ref = buffers[-1]
+            for k in range(size):
+                kept_ref[:, k, :, :] = piece_ref[k].reshape(rows // 2, 2, modes)
+            copies.append(
+                pltpu.make_async_copy(kept_ref, own_ref.at[:, momenta], sems.at[len(copies)])
+            )
+            copies[-1].start()
+    for copy in copies:
+        copy.wait()
+
+
+def project(index, factor, plan, pieces, total, count, earlier):
+    _, rows, modes = pieces[0].shape
     vmem = pl.BlockSpec(memory_space=pltpu.VMEM)
     kept = pl.BlockSpec(memory_space=pl.ANY)
-    step = first // size
+    own = [piece for piece, entry in zip(pieces, plan) if entry[:2] == (0, 0)]
+    buffers = [
+        pltpu.VMEM((rows // 2, piece.shape[0], 2, modes), jnp.bfloat16)
+        for piece in list(pieces) + own
+    ]
     return pl.pallas_call(
-        functools.partial(project_kernel, count=count),
-        grid=(1,),
+        functools.partial(project_kernel, plan=plan, count=count, aliased=len(earlier)),
         out_shape=[
             jax.ShapeDtypeStruct((rows // 2, total, 2, modes), jnp.bfloat16),
             jax.ShapeDtypeStruct((count, rows // 2, total, 2, modes), jnp.bfloat16),
         ],
         in_specs=[pl.BlockSpec(memory_space=pltpu.SMEM)]
-        + [vmem] * (1 + count)
+        + [vmem] * (1 + len(pieces))
         + [kept] * len(earlier),
-        out_specs=[
-            pl.BlockSpec((rows // 2, size, 2, modes), lambda i: (0, step, 0, 0)),
-            pl.BlockSpec((count, rows // 2, size, 2, modes), lambda i: (0, 0, step, 0, 0)),
-        ],
-        input_output_aliases={2 + count + i: i for i in range(len(earlier))},
+        out_specs=[kept, kept],
+        scratch_shapes=buffers + [pltpu.SemaphoreType.DMA((len(pieces) + len(own),))],
+        input_output_aliases={2 + len(pieces) + i: i for i in range(len(earlier))},
+        compiler_params=pltpu.CompilerParams(vmem_limit_bytes=24 << 20),
     )(index, *[in_vmem(v) for v in (factor, *pieces)], *earlier)
 
 
 def exchange(blocks, axis):
-    return [blocks[0]] + [shifted_2(blocks[by], axis, by) for by in range(1, len(blocks))]
+    length = len(blocks)
+    steps = sorted(range(1, length), key=lambda by: (min(by, length - by) == 1, by))
+    return [blocks[0]] + [shifted_2(blocks[by], axis, by) for by in steps]
 
 
 def paired(axis):
@@ -359,10 +380,23 @@
     factor = perambulators[0]
     flat_sum = owned_sum(flat_parts)
     flat_pieces = gather(flat_sum, "tm", False)
-    earlier = project(section, factor, flat_pieces, 3, 0, ())
+    section_count = lax.axis_size("tm")
+    order = section_order(section_count)
+    flat_plan = tuple((flip, by, 0) for flip, by in order)
+    deep_plan = tuple((flip, by, 2) for flip, by in order)
+    early = section_count if section_count % 2 else section_count // 2 + 1
+    earlier = project(section, factor, flat_plan[:early], flat_pieces[:early], 3, section_count, ())
     deep_sum = owned_sum(deep_parts)
     deep_pieces = gather(deep_sum, "tm", True)
-    own, projected = project(section, factor, deep_pieces, 3, 2, earlier)
+    own, projected = project(
+        section,
+        factor,
+        flat_plan[early:] + deep_plan,
+        flat_pieces[early:] + deep_pieces,
+        3,
+        section_count,
+        earlier,
+    )
     return (own[None], projected[None])
 
 

time: 69 us -> 68.9 us (level)
  starting transfers between devices: 19.9 us -> 20.6 us
  waiting for transfers between devices: 18.4 us -> 17.7 us
    ppermute x1, starting transfers between devices: 0.07 us -> 1.6 us  [gather(): lax.ppermute(shard, axis, [(((i ^ 1) + by) % length, i) for i in range(le...]
  transfers between devices with their start and end apart: 13 -> 13, of which waited for: 8 -> 5; matrix products, arithmetic and copies ran while one was open for 15% -> 15% of each run, Pallas kernels for 25% -> 25%
where the time goes in v2:
time: 68.9 us; the launch traced here: 68.6 us
  starting transfers between devices  20.6 us (30%)
  Pallas kernels  18 us (26%)
  waiting for transfers between devices  17.7 us (26%)
  other arithmetic  7.9 us (11%)
  local copies, waits for them, and re-layouts  3.61 us (5%)
  between operations  0.75 us (1%)
    ppermute x9, starting transfers between devices, shifted_2(): lax.ppermute(shard, axis, [(i, (i + by) % length) for i in range(length)])  18.5 us
    ppermute x9, waiting for transfers between devices, shifted_2(): lax.ppermute(shard, axis, [(i, (i + by) % length) for i in range(length)])  17.7 us
    pallas_call x1, Pallas kernels, contract_flat(): pl.pallas_call(functools.partial(flat_kernel, scale=scale), out_shape=[ou...  12.6 us
    mul x2, other arithmetic, phase_angle(): 2.0 * math.pi  5.84 us
    pallas_call x1, Pallas kernels, contract_deep(): pl.pallas_call(functools.partial(deep_kernel, scale=scale), out_shape=[ou...  3.12 us
    pallas_call x2, Pallas kernels, project(): pl.pallas_call(functools.partial(project_kernel, plan=plan, count=count,...  2.3 us
    slice x3, local copies, waits for them, and re-layouts, phase_angle(): weights[0] * first_pos / LX + weights[1] * second_pos / LY  1.99 us
    ppermute x1, starting transfers between devices, gather(): lax.ppermute(shard, axis, [(((i ^ 1) + by) % length, i) for i in range(le...  1.6 us
  transfers between devices with their start and end apart: 13, of which 5 were waited for; matrix products, arithmetic and copies ran while one was open for 15% of the time, Pallas kernels for 25%

profile of v2, /device:TPU:0, one launch (start us, length us, event | category | flops | bytes accessed | tf_op | source)
XLA Modules:
  0.0 68.6 jit_solution(2115643657429931274)
XLA Ops:
  0.6 5.1 %collective-permute-start.3 = (bf16[2,3,512,256]{3,2,1,0:T(8,128)(2,1)}, bf16[2,3,512,256]{3,2,1,0:T(8,128)(2,1)S(1)}, u32[]{:S(2)}, u32[]{:S(2)}) collective-permute-start(bf16[2,3,512,256]{3,2,1,0:T(8,128)(2,1)} %bitcast.34), channel_id=1, source_target_pairs={{0,3},{1,0},{2,1},{3,2},{4,7},{5,4},{6,5},{7,6},{8,11},{9,8},{10,9... | collective-permute-start | bytes 4718600 | tf_op jit(solution)/shard_map/ppermute | solution.py:18
  5.8 0.8 %slice_convert_fusion.2 = (f32[1,3]{1,0:T(1,128)S(1)}, f32[1,3]{1,0:T(1,128)S(1)}, f32[1,3]{1,0:T(1,128)S(1)}) fusion(s32[3,3]{1,0:T(4,128)} %param.6), kind=kLoop, calls=%fused_computation.32 | loop fusion | flops 9 | bytes 72 | tf_op jit(solution)/shard_map/convert_element_type | solution.py:22
  6.6 0.7 fusion.7
  7.2 1.9 %add_multiply_fusion.2 = f32[1,512]{1,0:T(1,128)S(1)} fusion(f32[]{:T(128)} %bitcast.5, f32[]{:T(128)} %bitcast.4, s32[]{:T(128)} %axis_index.25, f32[]{:T(128)} %bitcast.3), kind=kLoop, calls=%fused_computation.28 | loop fusion | flops 21504 | bytes 2064 | tf_op jit(solution)/shard_map/mul | solution.py:24
  9.2 0.7 fusion.9
  9.8 0.7 fusion.8
  10.5 3.9 %add_multiply_fusion = (f32[1,512]{1,0:T(1,128)S(1)}, f32[1,512]{1,0:T(1,128)S(1)}) fusion(f32[]{:T(128)} %bitcast.11, f32[]{:T(128)} %bitcast.10, f32[]{:T(128)} %bitcast.9, s32[]{:T(128)} %axis_index.25, f32[]{:T(128)} %bitcast.8, f32[]{:T(128)} %bitcast.7, f32[]{:T(128)} %bitcast.6), kind=kLoop, calls=%fused_computation.26 | loop fusion | flops 26112 | bytes 4124 | tf_op jit(solution)/shard_map/mul | solution.py:24
  14.4 0.1 fusion.1
  14.5 0.9 %bitcast_convert_fusion = f32[3,2,3,3,512]{4,1,3,2,0:T(2,128)S(1)} fusion(bf16[1,3,2,3,3,512]{5,2,4,3,1,0:T(2,128)(2,1)} %param.5), kind=kLoop, calls=%fused_computation.5 | loop fusion | flops 27648 | bytes 165888 | tf_op jit(solution)/shard_map/convert_element_type | solution.py:46
  15.3 0.1 multiply_add_fusion
  15.5 0.1 pad_maximum_fusion
  15.6 0.1 reshape.320
  15.7 0.1 copy.9
  15.8 0.0 copy-start.1
  15.8 1.4 %copy-done.1 = bf16[1,2,3,512,256]{4,3,2,1,0:T(8,128)(2,1)S(1)} copy-done((bf16[1,2,3,512,256]{4,3,2,1,0:T(8,128)(2,1)S(1)}, bf16[1,2,3,512,256]{4,3,2,1,0:T(8,128)(2,1)}, u32[]{:S(2)}) %copy-start.1) | copy-done | bytes 1572888
  17.2 12.6 %contract_xy.1 = (bf16[2,128,256]{2,1,0:T(8,128)(2,1)S(1)}, bf16[2,128,256]{2,1,0:T(8,128)(2,1)S(1)}, bf16[2,128,256]{2,1,0:T(8,128)(2,1)S(1)}, bf16[2,128,256]{...) custom-call(s32[1]{0:T(128)} %bitcast.2.index_ref, f32[512,54]{1,0:T(8,128)S(1)} %bitcast.33, ...), custom_call_target="tpu_custom_call" | custom-call | flops 2415919104 | bytes 3145728 | tf_op jit(solution)/shard_map/contract_xy/pallas_call | solution.py:200
  29.8 0.1 collective-permute-start
  29.9 1.0 %collective-permute-start.1 = (bf16[2,128,256]{2,1,0:T(8,128)(2,1)S(1)}, bf16[2,128,256]{2,1,0:T(8,128)(2,1)S(1)}, u32[]{:S(2)}, u32[]{:S(2)}) collective-permute-start(bf16[2,128,256]{2,1,0:T(8,128)(2,1)S(1)} %get-tuple-element.22), channel_id=1, source_target_pairs={{0,1},{1,2},{2,3},{3,0},{4,5},{5,6},{6,7},{7,4},{8,9},{9,10},{10,1... | collective-permute-start | bytes 393224 | tf_op jit(solution)/shard_map/ppermute | solution.py:18
  30.9 2.9 %collective-permute-start.2 = (bf16[2,128,256]{2,1,0:T(8,128)(2,1)S(1)}, bf16[2,128,256]{2,1,0:T(8,128)(2,1)S(1)}, u32[]{:S(2)}, u32[]{:S(2)}) collective-permute-start(bf16[2,128,256]{2,1,0:T(8,128)(2,1)S(1)} %get-tuple-element.23), channel_id=1, source_target_pairs={{0,3},{1,0},{2,1},{3,2},{4,7},{5,4},{6,5},{7,6},{8,11},{9,8},{10,9... | collective-permute-start | bytes 393224 | tf_op jit(solution)/shard_map/ppermute | solution.py:18
  33.7 7.2 %collective-permute-done.3.source_ref = bf16[2,3,512,256]{3,2,1,0:T(8,128)(2,1)S(1)} collective-permute-done((bf16[2,3,512,256]{3,2,1,0:T(8,128)(2,1)}, bf16[2,3,512,256]{3,2,1,0:T(8,128)(2,1)S(1)}, u32[]{:S(2)}, u32[]{:S(2)}) %collective-permute-start.3) | collective-permute-done | bytes 1572896 | tf_op jit(solution)/shard_map/ppermute | solution.py:18
  40.9 0.0 copy-start
  40.9 3.1 %contract_z.1 = (bf16[1,128,256]{2,1,0:T(8,128)(2,1)S(1)}, bf16[1,128,256]{2,1,0:T(8,128)(2,1)S(1)}, bf16[1,128,256]{2,1,0:T(8,128)(2,1)S(1)}, bf16[1,128,256]{2,1,0:T(8,128)(2,1)S(1)}) custom-call(s32[1]{0:T(128)} %bitcast.2.index_ref, bf16[512,3072]{1,0:T(8,128)(2,1)S(1)} %get-tuple-element.24.left_ref, ...), custom_call_target="tpu_custom_call" | custom-call | flops 805306368 | bytes 1572864 | tf_op jit(solution)/shard_map/contract_z/pallas_call | solution.py:226
  44.1 5.0 %collective-permute-done = bf16[2,128,256]{2,1,0:T(8,128)(2,1)S(1)} collective-permute-done((bf16[2,128,256]{2,1,0:T(8,128)(2,1)S(1)}, bf16[2,128,256]{2,1,0:T(8,128)(2,1)S(1)}, u32[]{:S(2)}, u32[]{:S(2)}) %collective-permute-start) | collective-permute-done | bytes 131104 | tf_op jit(solution)/shard_map/ppermute | solution.py:18
  49.1 0.0 collective-permute-done.1
  49.1 0.0 collective-permute-done.2
  49.1 0.1 add_convert_fusion.rest_0_
  49.2 1.6 %collective-permute-start.4 = (bf16[2,128,256]{2,1,0:T(8,128)(2,1)S(1)}, bf16[2,128,256]{2,1,0:T(8,128)(2,1)S(1)}, u32[]{:S(2)}, u32[]{:S(2)}) collective-permute-start(bf16[2,128,256]{2,1,0:T(8,128)(2,1)S(1)} %add_convert_fusion.rest_0_), channel_id=1, source_target_pairs={{0,8},{4,12},{8,0},{12,4},{1,9},{5,13},{9,1},{13,5},{2,10},{6,14},... | collective-permute-start | bytes 393224 | tf_op jit(solution)/shard_map/ppermute | solution.py:18
  50.7 3.4 %collective-permute-start.8 = (bf16[1,128,256]{2,1,0:T(8,128)(2,1)S(1)}, bf16[1,128,256]{2,1,0:T(8,128)(2,1)S(1)}, u32[]{:S(2)}, u32[]{:S(2)}) collective-permute-start(bf16[1,128,256]{2,1,0:T(8,128)(2,1)S(1)} %get-tuple-element.29), channel_id=1, source_target_pairs={{0,3},{1,0},{2,1},{3,2},{4,7},{5,4},{6,5},{7,6},{8,11},{9,8},{10,9... | collective-permute-start | bytes 196616 | tf_op jit(solution)/shard_map/ppermute | solution.py:18
  54.1 0.0 collective-permute-start.7
  54.1 3.8 %collective-permute-start.6 = (bf16[1,128,256]{2,1,0:T(8,128)(2,1)S(1)}, bf16[1,128,256]{2,1,0:T(8,128)(2,1)S(1)}, u32[]{:S(2)}, u32[]{:S(2)}) collective-permute-start(bf16[1,128,256]{2,1,0:T(8,128)(2,1)S(1)} %get-tuple-element.28), channel_id=1, source_target_pairs={{0,2},{1,3},{2,0},{3,1},{4,6},{5,7},{6,4},{7,5},{8,10},{9,11},{10,... | collective-permute-start | bytes 196616 | tf_op jit(solution)/shard_map/ppermute | solution.py:18
  57.9 0.0 collective-permute-start.12
  57.9 0.0 collective-permute-done.4.rest_1_
  57.9 0.5 collective-permute-start.5
  58.5 0.0 collective-permute-done.8
  58.5 2.7 %collective-permute-done.7 = bf16[1,128,256]{2,1,0:T(8,128)(2,1)S(1)} collective-permute-done((bf16[1,128,256]{2,1,0:T(8,128)(2,1)S(1)}, bf16[1,128,256]{2,1,0:T(8,128)(2,1)S(1)}, u32[]{:S(2)}, u32[]{:S(2)}) %collective-permute-start.7) | collective-permute-done | bytes 65568 | tf_op jit(solution)/shard_map/ppermute | solution.py:18
  61.2 1.2 %collective-permute-done.6 = bf16[1,128,256]{2,1,0:T(8,128)(2,1)S(1)} collective-permute-done((bf16[1,128,256]{2,1,0:T(8,128)(2,1)S(1)}, bf16[1,128,256]{2,1,0:T(8,128)(2,1)S(1)}, u32[]{:S(2)}, u32[]{:S(2)}) %collective-permute-start.6) | collective-permute-done | bytes 65568 | tf_op jit(solution)/shard_map/ppermute | solution.py:18
  62.4 0.6 collective-permute-start.9
  63.0 0.0 collective-permute-start.10
  63.0 1.6 %collective-permute-start.11 = (bf16[1,128,256]{2,1,0:T(8,128)(2,1)S(1)}, bf16[1,128,256]{2,1,0:T(8,128)(2,1)S(1)}, u32[]{:S(2)}, u32[]{:S(2)}) collective-permute-start(bf16[1,128,256]{2,1,0:T(8,128)(2,1)S(1)} %add_convert_fusion.1.rest_1_), channel_id=1, source_target_pairs={{12,0},{8,4},{4,8},{0,12},{13,1},{9,5},{5,9},{1,13},{14,2},{10,6},... | collective-permute-start | bytes 196616 | tf_op jit(solution)/shard_map/ppermute | solution.py:354
  64.6 0.0 collective-permute-done.12.rest_2_
  64.6 0.0 copy-done
  64.6 1.2 %shard_map.59 = (bf16[64,3,2,256]{3,2,1,0:T(2,128)(2,1)}, bf16[4,64,3,2,256]{4,3,2,1,0:T(2,128)(2,1)}) custom-call(s32[1]{0:T(128)} %bitcast.index_ref, bf16[2,256,256]{2,1,0:T(8,128)(2,1)S(1)} %bitcast.31, bf16[2,128,256]{2,1,0:T(8,128)(2,1)S(1)} %add_convert_fusion.rest_0_, bf16[2,128,256]{2,1,0:T(8,128)(2,1)S(1)} %collective-permute-done.4.rest_1_, ...), custom_call_target="tpu_custom_call" | custom-call | tf_op jit(solution)/shard_map/pallas_call | solution.py:313
  65.8 1.6 %collective-permute-done.9.rest_2_ = bf16[1,128,256]{2,1,0:T(8,128)(2,1)S(1)} collective-permute-done((bf16[1,128,256]{2,1,0:T(8,128)(2,1)S(1)}, bf16[1,128,256]{2,1,0:T(8,128)(2,1)S(1)}, u32[]{:S(2)}, u32[]{:S(2)}) %collective-permute-start.9) | collective-permute-done | bytes 65568 | tf_op jit(solution)/shard_map/ppermute | solution.py:18
  67.4 0.0 collective-permute-done.10.rest_3_
  67.4 0.0 collective-permute-done.11.rest_4_
  67.4 0.0 collective-permute-done.5.rest_0_
  67.4 1.1 %shard_map.60 = (bf16[64,3,2,256]{3,2,1,0:T(2,128)(2,1)}, bf16[4,64,3,2,256]{4,3,2,1,0:T(2,128)(2,1)}) custom-call(s32[1]{0:T(128)} %bitcast.index_ref, bf16[2,256,256]{2,1,0:T(8,128)(2,1)S(1)} %bitcast.32, bf16[2,128,256]{2,1,0:T(8,128)(2,1)S(1)} %collective-permute-done.5.rest_0_, ...), custom_call_target="tpu_custom_call", output_to_operand_aliasing={{0}: (7, {}), {1}: (8, {})} | custom-call | tf_op jit(solution)/shard_map/pallas_call | solution.py:313
  (1 shorter events, 0.0 us)
Async XLA Ops:
  0.6 40.3 %collective-permute-start.3 = (bf16[2,3,512,256]{3,2,1,0:T(8,128)(2,1)}, bf16[2,3,512,256]{3,2,1,0:T(8,128)(2,1)S(1)}, u32[]{:S(2)}, u32[]{:S(2)}) collective-permute-start(bf16[2,3,512,256]{3,2,1,0:T(8,128)(2,1)} %bitcast.34), channel_id=1, source_target_pairs={{0,3},{1,0},{2,1},{3,2},{4,7},{5,4},{6,5},{7,6},{8,11},{9,8},{10,9... | collective-permute-start | bytes 4718600 | tf_op jit(solution)/shard_map/ppermute | solution.py:18
  15.8 1.4 %copy-start.1 = (bf16[1,2,3,512,256]{4,3,2,1,0:T(8,128)(2,1)S(1)}, bf16[1,2,3,512,256]{4,3,2,1,0:T(8,128)(2,1)}, u32[]{:S(2)}) copy-start(bf16[1,2,3,512,256]{4,3,2,1,0:T(8,128)(2,1)} %param.4) | copy-start | bytes 4718596
  29.8 19.3 %collective-permute-start = (bf16[2,128,256]{2,1,0:T(8,128)(2,1)S(1)}, bf16[2,128,256]{2,1,0:T(8,128)(2,1)S(1)}, u32[]{:S(2)}, u32[]{:S(2)}) collective-permute-start(bf16[2,128,256]{2,1,0:T(8,128)(2,1)S(1)} %get-tuple-element.21), channel_id=1, source_target_pairs={{0,2},{1,3},{2,0},{3,1},{4,6},{5,7},{6,4},{7,5},{8,10},{9,11},{10,... | collective-permute-start | bytes 393224 | tf_op jit(solution)/shard_map/ppermute | solution.py:18
  29.9 19.2 %collective-permute-start.1 = (bf16[2,128,256]{2,1,0:T(8,128)(2,1)S(1)}, bf16[2,128,256]{2,1,0:T(8,128)(2,1)S(1)}, u32[]{:S(2)}, u32[]{:S(2)}) collective-permute-start(bf16[2,128,256]{2,1,0:T(8,128)(2,1)S(1)} %get-tuple-element.22), channel_id=1, source_target_pairs={{0,1},{1,2},{2,3},{3,0},{4,5},{5,6},{6,7},{7,4},{8,9},{9,10},{10,1... | collective-permute-start | bytes 393224 | tf_op jit(solution)/shard_map/ppermute | solution.py:18
  30.9 18.2 %collective-permute-start.2 = (bf16[2,128,256]{2,1,0:T(8,128)(2,1)S(1)}, bf16[2,128,256]{2,1,0:T(8,128)(2,1)S(1)}, u32[]{:S(2)}, u32[]{:S(2)}) collective-permute-start(bf16[2,128,256]{2,1,0:T(8,128)(2,1)S(1)} %get-tuple-element.23), channel_id=1, source_target_pairs={{0,3},{1,0},{2,1},{3,2},{4,7},{5,4},{6,5},{7,6},{8,11},{9,8},{10,9... | collective-permute-start | bytes 393224 | tf_op jit(solution)/shard_map/ppermute | solution.py:18
  40.9 23.7 %copy-start = (bf16[1,2,256,256]{3,2,1,0:T(8,128)(2,1)S(1)}, bf16[1,2,256,256]{3,2,1,0:T(8,128)(2,1)}, u32[]{:S(2)}) copy-start(bf16[1,2,256,256]{3,2,1,0:T(8,128)(2,1)} %param.7) | copy-start | bytes 786436
  49.2 8.8 %collective-permute-start.4 = (bf16[2,128,256]{2,1,0:T(8,128)(2,1)S(1)}, bf16[2,128,256]{2,1,0:T(8,128)(2,1)S(1)}, u32[]{:S(2)}, u32[]{:S(2)}) collective-permute-start(bf16[2,128,256]{2,1,0:T(8,128)(2,1)S(1)} %add_convert_fusion.rest_0_), channel_id=1, source_target_pairs={{0,8},{4,12},{8,0},{12,4},{1,9},{5,13},{9,1},{13,5},{2,10},{6,14},... | collective-permute-start | bytes 393224 | tf_op jit(solution)/shard_map/ppermute | solution.py:18
  50.7 7.8 %collective-permute-start.8 = (bf16[1,128,256]{2,1,0:T(8,128)(2,1)S(1)}, bf16[1,128,256]{2,1,0:T(8,128)(2,1)S(1)}, u32[]{:S(2)}, u32[]{:S(2)}) collective-permute-start(bf16[1,128,256]{2,1,0:T(8,128)(2,1)S(1)} %get-tuple-element.29), channel_id=1, source_target_pairs={{0,3},{1,0},{2,1},{3,2},{4,7},{5,4},{6,5},{7,6},{8,11},{9,8},{10,9... | collective-permute-start | bytes 196616 | tf_op jit(solution)/shard_map/ppermute | solution.py:18
  54.1 7.1 %collective-permute-start.7 = (bf16[1,128,256]{2,1,0:T(8,128)(2,1)S(1)}, bf16[1,128,256]{2,1,0:T(8,128)(2,1)S(1)}, u32[]{:S(2)}, u32[]{:S(2)}) collective-permute-start(bf16[1,128,256]{2,1,0:T(8,128)(2,1)S(1)} %get-tuple-element.27), channel_id=1, source_target_pairs={{0,1},{1,2},{2,3},{3,0},{4,5},{5,6},{6,7},{7,4},{8,9},{9,10},{10,1... | collective-permute-start | bytes 196616 | tf_op jit(solution)/shard_map/ppermute | solution.py:18
  54.1 8.2 %collective-permute-start.6 = (bf16[1,128,256]{2,1,0:T(8,128)(2,1)S(1)}, bf16[1,128,256]{2,1,0:T(8,128)(2,1)S(1)}, u32[]{:S(2)}, u32[]{:S(2)}) collective-permute-start(bf16[1,128,256]{2,1,0:T(8,128)(2,1)S(1)} %get-tuple-element.28), channel_id=1, source_target_pairs={{0,2},{1,3},{2,0},{3,1},{4,6},{5,7},{6,4},{7,5},{8,10},{9,11},{10,... | collective-permute-start | bytes 196616 | tf_op jit(solution)/shard_map/ppermute | solution.py:18
  57.9 6.7 %collective-permute-start.12 = (bf16[2,128,256]{2,1,0:T(8,128)(2,1)S(1)}, bf16[2,128,256]{2,1,0:T(8,128)(2,1)S(1)}, u32[]{:S(2)}, u32[]{:S(2)}) collective-permute-start(bf16[2,128,256]{2,1,0:T(8,128)(2,1)S(1)} %add_convert_fusion.rest_0_), channel_id=1, source_target_pairs={{0,4},{4,0},{8,12},{12,8},{1,5},{5,1},{9,13},{13,9},{2,6},{6,2},{1... | collective-permute-start | bytes 393224 | tf_op jit(solution)/shard_map/ppermute | solution.py:357
  57.9 9.5 %collective-permute-start.5 = (bf16[2,128,256]{2,1,0:T(8,128)(2,1)S(1)}, bf16[2,128,256]{2,1,0:T(8,128)(2,1)S(1)}, u32[]{:S(2)}, u32[]{:S(2)}) collective-permute-start(bf16[2,128,256]{2,1,0:T(8,128)(2,1)S(1)} %collective-permute-done.4.rest_1_), channel_id=1, source_target_pairs={{0,4},{4,0},{8,12},{12,8},{1,5},{5,1},{9,13},{13,9},{2,6},{6,2},{1... | collective-permute-start | bytes 393224 | tf_op jit(solution)/shard_map/ppermute | solution.py:360
  62.4 5.0 %collective-permute-start.9 = (bf16[1,128,256]{2,1,0:T(8,128)(2,1)S(1)}, bf16[1,128,256]{2,1,0:T(8,128)(2,1)S(1)}, u32[]{:S(2)}, u32[]{:S(2)}) collective-permute-start(bf16[1,128,256]{2,1,0:T(8,128)(2,1)S(1)} %add_convert_fusion.1.rest_1_), channel_id=1, source_target_pairs={{0,8},{4,12},{8,0},{12,4},{1,9},{5,13},{9,1},{13,5},{2,10},{6,14},... | collective-permute-start | bytes 196616 | tf_op jit(solution)/shard_map/ppermute | solution.py:18
  63.0 4.4 %collective-permute-start.10 = (bf16[1,128,256]{2,1,0:T(8,128)(2,1)S(1)}, bf16[1,128,256]{2,1,0:T(8,128)(2,1)S(1)}, u32[]{:S(2)}, u32[]{:S(2)}) collective-permute-start(bf16[1,128,256]{2,1,0:T(8,128)(2,1)S(1)} %add_convert_fusion.1.rest_1_), channel_id=1, source_target_pairs={{0,4},{4,0},{8,12},{12,8},{1,5},{5,1},{9,13},{13,9},{2,6},{6,2},{1... | collective-permute-start | bytes 196616 | tf_op jit(solution)/shard_map/ppermute | solution.py:357
  63.0 4.4 %collective-permute-start.11 = (bf16[1,128,256]{2,1,0:T(8,128)(2,1)S(1)}, bf16[1,128,256]{2,1,0:T(8,128)(2,1)S(1)}, u32[]{:S(2)}, u32[]{:S(2)}) collective-permute-start(bf16[1,128,256]{2,1,0:T(8,128)(2,1)S(1)} %add_convert_fusion.1.rest_1_), channel_id=1, source_target_pairs={{12,0},{8,4},{4,8},{0,12},{13,1},{9,5},{5,9},{1,13},{14,2},{10,6},... | collective-permute-start | bytes 196616 | tf_op jit(solution)/shard_map/ppermute | solution.py:354

commit v3 on v2

--- a/solution.py
+++ b/solution.py
@@ -326,9 +326,11 @@
     )(index, *[in_vmem(v) for v in (factor, *pieces)], *earlier)
 
 
-def exchange(blocks, axis):
+def exchange(blocks, axis, far_last):
     length = len(blocks)
-    steps = sorted(range(1, length), key=lambda by: (min(by, length - by) == 1, by))
+    steps = range(1, length)
+    if far_last:
+        steps = sorted(steps, key=lambda by: (min(by, length - by) == 1, by))
     return [blocks[0]] + [shifted_2(blocks[by], axis, by) for by in steps]
 
 
@@ -373,10 +375,10 @@
     section = lax.axis_index("tm").astype(jnp.int32).reshape(1)
     *flat, left, wide = contract_flat(tile, weights, vectors, tile_count, scale)
     raised = jnp.concatenate([vectors[:, :, plane:], forward], 2)
-    flat_parts = exchange(flat, "space")
+    flat_parts = exchange(flat, "space", True)
     deep = contract_deep(tile, left, wide, raised, tile_count, scale)
     flat_parts, _ = lax.optimization_barrier((flat_parts, deep))
-    deep_parts = exchange(deep, "space")
+    deep_parts = exchange(deep, "space", False)
     factor = perambulators[0]
     flat_sum = owned_sum(flat_parts)
     flat_pieces = gather(flat_sum, "tm", False)

time: 68.9 us -> 68.6 us (level)
  transfers between devices with their start and end apart: 13 -> 13, of which waited for: 5 -> 4; matrix products, arithmetic and copies ran while one was open for 15% -> 15% of each run, Pallas kernels for 25% -> 25%
where the time goes in v3:
time: 68.6 us; the launch traced here: 68.3 us
  starting transfers between devices  20.6 us (30%)
  Pallas kernels  18 us (26%)
  waiting for transfers between devices  17.5 us (26%)
  other arithmetic  7.9 us (12%)
  local copies, waits for them, and re-layouts  3.61 us (5%)
  between operations  0.75 us (1%)
    ppermute x9, starting transfers between devices, shifted_2(): lax.ppermute(shard, axis, [(i, (i + by) % length) for i in range(length)])  18.5 us
    ppermute x9, waiting for transfers between devices, shifted_2(): lax.ppermute(shard, axis, [(i, (i + by) % length) for i in range(length)])  17.5 us
    pallas_call x1, Pallas kernels, contract_flat(): pl.pallas_call(functools.partial(flat_kernel, scale=scale), out_shape=[ou...  12.6 us
    mul x2, other arithmetic, phase_angle(): 2.0 * math.pi  5.84 us
    pallas_call x1, Pallas kernels, contract_deep(): pl.pallas_call(functools.partial(deep_kernel, scale=scale), out_shape=[ou...  3.12 us
    pallas_call x2, Pallas kernels, project(): pl.pallas_call(functools.partial(project_kernel, plan=plan, count=count,...  2.3 us
    slice x3, local copies, waits for them, and re-layouts, phase_angle(): weights[0] * first_pos / LX + weights[1] * second_pos / LY  1.99 us
    ppermute x1, starting transfers between devices, gather(): lax.ppermute(shard, axis, [(((i ^ 1) + by) % length, i) for i in range(le...  1.6 us
  transfers between devices with their start and end apart: 13, of which 4 were waited for; matrix products, arithmetic and copies ran while one was open for 15% of the time, Pallas kernels for 25%

profile of v3, /device:TPU:0, one launch (start us, length us, event | category | flops | bytes accessed | tf_op | source)
XLA Modules:
  0.0 68.3 jit_solution(7427701124567791971)
XLA Ops:
  0.6 5.1 %collective-permute-start.3 = (bf16[2,3,512,256]{3,2,1,0:T(8,128)(2,1)}, bf16[2,3,512,256]{3,2,1,0:T(8,128)(2,1)S(1)}, u32[]{:S(2)}, u32[]{:S(2)}) collective-permute-start(bf16[2,3,512,256]{3,2,1,0:T(8,128)(2,1)} %bitcast.34), channel_id=1, source_target_pairs={{0,3},{1,0},{2,1},{3,2},{4,7},{5,4},{6,5},{7,6},{8,11},{9,8},{10,9... | collective-permute-start | bytes 4718600 | tf_op jit(solution)/shard_map/ppermute | solution.py:18
  5.8 0.8 %slice_convert_fusion.2 = (f32[1,3]{1,0:T(1,128)S(1)}, f32[1,3]{1,0:T(1,128)S(1)}, f32[1,3]{1,0:T(1,128)S(1)}) fusion(s32[3,3]{1,0:T(4,128)} %param.6), kind=kLoop, calls=%fused_computation.32 | loop fusion | flops 9 | bytes 72 | tf_op jit(solution)/shard_map/convert_element_type | solution.py:22
  6.6 0.7 fusion.7
  7.2 1.9 %add_multiply_fusion.2 = f32[1,512]{1,0:T(1,128)S(1)} fusion(f32[]{:T(128)} %bitcast.5, f32[]{:T(128)} %bitcast.4, s32[]{:T(128)} %axis_index.25, f32[]{:T(128)} %bitcast.3), kind=kLoop, calls=%fused_computation.28 | loop fusion | flops 21504 | bytes 2064 | tf_op jit(solution)/shard_map/mul | solution.py:24
  9.2 0.7 fusion.9
  9.8 0.7 fusion.8
  10.5 3.9 %add_multiply_fusion = (f32[1,512]{1,0:T(1,128)S(1)}, f32[1,512]{1,0:T(1,128)S(1)}) fusion(f32[]{:T(128)} %bitcast.11, f32[]{:T(128)} %bitcast.10, f32[]{:T(128)} %bitcast.9, s32[]{:T(128)} %axis_index.25, f32[]{:T(128)} %bitcast.8, f32[]{:T(128)} %bitcast.7, f32[]{:T(128)} %bitcast.6), kind=kLoop, calls=%fused_computation.26 | loop fusion | flops 26112 | bytes 4124 | tf_op jit(solution)/shard_map/mul | solution.py:24
  14.4 0.1 fusion.1
  14.5 0.9 %bitcast_convert_fusion = f32[3,2,3,3,512]{4,1,3,2,0:T(2,128)S(1)} fusion(bf16[1,3,2,3,3,512]{5,2,4,3,1,0:T(2,128)(2,1)} %param.5), kind=kLoop, calls=%fused_computation.5 | loop fusion | flops 27648 | bytes 165888 | tf_op jit(solution)/shard_map/convert_element_type | solution.py:46
  15.3 0.1 multiply_add_fusion
  15.5 0.1 pad_maximum_fusion
  15.6 0.1 reshape.320
  15.7 0.1 copy.9
  15.8 0.0 copy-start.1
  15.8 1.4 %copy-done.1 = bf16[1,2,3,512,256]{4,3,2,1,0:T(8,128)(2,1)S(1)} copy-done((bf16[1,2,3,512,256]{4,3,2,1,0:T(8,128)(2,1)S(1)}, bf16[1,2,3,512,256]{4,3,2,1,0:T(8,128)(2,1)}, u32[]{:S(2)}) %copy-start.1) | copy-done | bytes 1572888
  17.2 12.6 %contract_xy.1 = (bf16[2,128,256]{2,1,0:T(8,128)(2,1)S(1)}, bf16[2,128,256]{2,1,0:T(8,128)(2,1)S(1)}, bf16[2,128,256]{2,1,0:T(8,128)(2,1)S(1)}, bf16[2,128,256]{...) custom-call(s32[1]{0:T(128)} %bitcast.2.index_ref, f32[512,54]{1,0:T(8,128)S(1)} %bitcast.33, ...), custom_call_target="tpu_custom_call" | custom-call | flops 2415919104 | bytes 3145728 | tf_op jit(solution)/shard_map/contract_xy/pallas_call | solution.py:200
  29.8 0.1 collective-permute-start
  29.9 1.0 %collective-permute-start.1 = (bf16[2,128,256]{2,1,0:T(8,128)(2,1)S(1)}, bf16[2,128,256]{2,1,0:T(8,128)(2,1)S(1)}, u32[]{:S(2)}, u32[]{:S(2)}) collective-permute-start(bf16[2,128,256]{2,1,0:T(8,128)(2,1)S(1)} %get-tuple-element.22), channel_id=1, source_target_pairs={{0,1},{1,2},{2,3},{3,0},{4,5},{5,6},{6,7},{7,4},{8,9},{9,10},{10,1... | collective-permute-start | bytes 393224 | tf_op jit(solution)/shard_map/ppermute | solution.py:18
  30.9 2.9 %collective-permute-start.2 = (bf16[2,128,256]{2,1,0:T(8,128)(2,1)S(1)}, bf16[2,128,256]{2,1,0:T(8,128)(2,1)S(1)}, u32[]{:S(2)}, u32[]{:S(2)}) collective-permute-start(bf16[2,128,256]{2,1,0:T(8,128)(2,1)S(1)} %get-tuple-element.23), channel_id=1, source_target_pairs={{0,3},{1,0},{2,1},{3,2},{4,7},{5,4},{6,5},{7,6},{8,11},{9,8},{10,9... | collective-permute-start | bytes 393224 | tf_op jit(solution)/shard_map/ppermute | solution.py:18
  33.7 7.2 %collective-permute-done.3.source_ref = bf16[2,3,512,256]{3,2,1,0:T(8,128)(2,1)S(1)} collective-permute-done((bf16[2,3,512,256]{3,2,1,0:T(8,128)(2,1)}, bf16[2,3,512,256]{3,2,1,0:T(8,128)(2,1)S(1)}, u32[]{:S(2)}, u32[]{:S(2)}) %collective-permute-start.3) | collective-permute-done | bytes 1572896 | tf_op jit(solution)/shard_map/ppermute | solution.py:18
  40.9 0.0 copy-start
  40.9 3.1 %contract_z.1 = (bf16[1,128,256]{2,1,0:T(8,128)(2,1)S(1)}, bf16[1,128,256]{2,1,0:T(8,128)(2,1)S(1)}, bf16[1,128,256]{2,1,0:T(8,128)(2,1)S(1)}, bf16[1,128,256]{2,1,0:T(8,128)(2,1)S(1)}) custom-call(s32[1]{0:T(128)} %bitcast.2.index_ref, bf16[512,3072]{1,0:T(8,128)(2,1)S(1)} %get-tuple-element.24.left_ref, ...), custom_call_target="tpu_custom_call" | custom-call | flops 805306368 | bytes 1572864 | tf_op jit(solution)/shard_map/contract_z/pallas_call | solution.py:226
  44.1 5.0 %collective-permute-done = bf16[2,128,256]{2,1,0:T(8,128)(2,1)S(1)} collective-permute-done((bf16[2,128,256]{2,1,0:T(8,128)(2,1)S(1)}, bf16[2,128,256]{2,1,0:T(8,128)(2,1)S(1)}, u32[]{:S(2)}, u32[]{:S(2)}) %collective-permute-start) | collective-permute-done | bytes 131104 | tf_op jit(solution)/shard_map/ppermute | solution.py:18
  49.1 0.0 collective-permute-done.1
  49.1 0.0 collective-permute-done.2
  49.1 0.1 add_convert_fusion.rest_0_
  49.2 1.6 %collective-permute-start.4 = (bf16[2,128,256]{2,1,0:T(8,128)(2,1)S(1)}, bf16[2,128,256]{2,1,0:T(8,128)(2,1)S(1)}, u32[]{:S(2)}, u32[]{:S(2)}) collective-permute-start(bf16[2,128,256]{2,1,0:T(8,128)(2,1)S(1)} %add_convert_fusion.rest_0_), channel_id=1, source_target_pairs={{0,8},{4,12},{8,0},{12,4},{1,9},{5,13},{9,1},{13,5},{2,10},{6,14},... | collective-permute-start | bytes 393224 | tf_op jit(solution)/shard_map/ppermute | solution.py:18
  50.7 3.4 %collective-permute-start.8 = (bf16[1,128,256]{2,1,0:T(8,128)(2,1)S(1)}, bf16[1,128,256]{2,1,0:T(8,128)(2,1)S(1)}, u32[]{:S(2)}, u32[]{:S(2)}) collective-permute-start(bf16[1,128,256]{2,1,0:T(8,128)(2,1)S(1)} %get-tuple-element.29), channel_id=1, source_target_pairs={{0,3},{1,0},{2,1},{3,2},{4,7},{5,4},{6,5},{7,6},{8,11},{9,8},{10,9... | collective-permute-start | bytes 196616 | tf_op jit(solution)/shard_map/ppermute | solution.py:18
  54.1 1.8 %collective-permute-start.7 = (bf16[1,128,256]{2,1,0:T(8,128)(2,1)S(1)}, bf16[1,128,256]{2,1,0:T(8,128)(2,1)S(1)}, u32[]{:S(2)}, u32[]{:S(2)}) collective-permute-start(bf16[1,128,256]{2,1,0:T(8,128)(2,1)S(1)} %get-tuple-element.28), channel_id=1, source_target_pairs={{0,2},{1,3},{2,0},{3,1},{4,6},{5,7},{6,4},{7,5},{8,10},{9,11},{10,... | collective-permute-start | bytes 196616 | tf_op jit(solution)/shard_map/ppermute | solution.py:18
  55.9 2.0 %collective-permute-start.6 = (bf16[1,128,256]{2,1,0:T(8,128)(2,1)S(1)}, bf16[1,128,256]{2,1,0:T(8,128)(2,1)S(1)}, u32[]{:S(2)}, u32[]{:S(2)}) collective-permute-start(bf16[1,128,256]{2,1,0:T(8,128)(2,1)S(1)} %get-tuple-element.27), channel_id=1, source_target_pairs={{0,1},{1,2},{2,3},{3,0},{4,5},{5,6},{6,7},{7,4},{8,9},{9,10},{10,1... | collective-permute-start | bytes 196616 | tf_op jit(solution)/shard_map/ppermute | solution.py:18
  57.9 0.0 collective-permute-start.12
  57.9 0.0 collective-permute-done.4.rest_1_
  57.9 0.5 collective-permute-start.5
  58.5 0.0 collective-permute-done.8
  58.5 3.7 %collective-permute-done.7 = bf16[1,128,256]{2,1,0:T(8,128)(2,1)S(1)} collective-permute-done((bf16[1,128,256]{2,1,0:T(8,128)(2,1)S(1)}, bf16[1,128,256]{2,1,0:T(8,128)(2,1)S(1)}, u32[]{:S(2)}, u32[]{:S(2)}) %collective-permute-start.7) | collective-permute-done | bytes 65568 | tf_op jit(solution)/shard_map/ppermute | solution.py:18
  62.1 0.0 collective-permute-done.6
  62.2 0.6 collective-permute-start.9
  62.8 0.0 collective-permute-start.10
  62.8 1.6 %collective-permute-start.11 = (bf16[1,128,256]{2,1,0:T(8,128)(2,1)S(1)}, bf16[1,128,256]{2,1,0:T(8,128)(2,1)S(1)}, u32[]{:S(2)}, u32[]{:S(2)}) collective-permute-start(bf16[1,128,256]{2,1,0:T(8,128)(2,1)S(1)} %add_convert_fusion.1.rest_1_), channel_id=1, source_target_pairs={{12,0},{8,4},{4,8},{0,12},{13,1},{9,5},{5,9},{1,13},{14,2},{10,6},... | collective-permute-start | bytes 196616 | tf_op jit(solution)/shard_map/ppermute | solution.py:356
  64.4 0.0 collective-permute-done.12.rest_2_
  64.4 0.0 copy-done
  64.4 1.2 %shard_map.59 = (bf16[64,3,2,256]{3,2,1,0:T(2,128)(2,1)}, bf16[4,64,3,2,256]{4,3,2,1,0:T(2,128)(2,1)}) custom-call(s32[1]{0:T(128)} %bitcast.index_ref, bf16[2,256,256]{2,1,0:T(8,128)(2,1)S(1)} %bitcast.31, bf16[2,128,256]{2,1,0:T(8,128)(2,1)S(1)} %add_convert_fusion.rest_0_, bf16[2,128,256]{2,1,0:T(8,128)(2,1)S(1)} %collective-permute-done.4.rest_1_, ...), custom_call_target="tpu_custom_call" | custom-call | tf_op jit(solution)/shard_map/pallas_call | solution.py:313
  65.5 1.6 %collective-permute-done.9.rest_2_ = bf16[1,128,256]{2,1,0:T(8,128)(2,1)S(1)} collective-permute-done((bf16[1,128,256]{2,1,0:T(8,128)(2,1)S(1)}, bf16[1,128,256]{2,1,0:T(8,128)(2,1)S(1)}, u32[]{:S(2)}, u32[]{:S(2)}) %collective-permute-start.9) | collective-permute-done | bytes 65568 | tf_op jit(solution)/shard_map/ppermute | solution.py:18
  67.2 0.0 collective-permute-done.10.rest_3_
  67.2 0.0 collective-permute-done.11.rest_4_
  67.2 0.0 collective-permute-done.5.rest_0_
  67.2 1.1 %shard_map.60 = (bf16[64,3,2,256]{3,2,1,0:T(2,128)(2,1)}, bf16[4,64,3,2,256]{4,3,2,1,0:T(2,128)(2,1)}) custom-call(s32[1]{0:T(128)} %bitcast.index_ref, bf16[2,256,256]{2,1,0:T(8,128)(2,1)S(1)} %bitcast.32, bf16[2,128,256]{2,1,0:T(8,128)(2,1)S(1)} %collective-permute-done.5.rest_0_, ...), custom_call_target="tpu_custom_call", output_to_operand_aliasing={{0}: (7, {}), {1}: (8, {})} | custom-call | tf_op jit(solution)/shard_map/pallas_call | solution.py:313
  (1 shorter events, 0.0 us)
Async XLA Ops:
  0.6 40.3 %collective-permute-start.3 = (bf16[2,3,512,256]{3,2,1,0:T(8,128)(2,1)}, bf16[2,3,512,256]{3,2,1,0:T(8,128)(2,1)S(1)}, u32[]{:S(2)}, u32[]{:S(2)}) collective-permute-start(bf16[2,3,512,256]{3,2,1,0:T(8,128)(2,1)} %bitcast.34), channel_id=1, source_target_pairs={{0,3},{1,0},{2,1},{3,2},{4,7},{5,4},{6,5},{7,6},{8,11},{9,8},{10,9... | collective-permute-start | bytes 4718600 | tf_op jit(solution)/shard_map/ppermute | solution.py:18
  15.8 1.4 %copy-start.1 = (bf16[1,2,3,512,256]{4,3,2,1,0:T(8,128)(2,1)S(1)}, bf16[1,2,3,512,256]{4,3,2,1,0:T(8,128)(2,1)}, u32[]{:S(2)}) copy-start(bf16[1,2,3,512,256]{4,3,2,1,0:T(8,128)(2,1)} %param.4) | copy-start | bytes 4718596
  29.8 19.3 %collective-permute-start = (bf16[2,128,256]{2,1,0:T(8,128)(2,1)S(1)}, bf16[2,128,256]{2,1,0:T(8,128)(2,1)S(1)}, u32[]{:S(2)}, u32[]{:S(2)}) collective-permute-start(bf16[2,128,256]{2,1,0:T(8,128)(2,1)S(1)} %get-tuple-element.21), channel_id=1, source_target_pairs={{0,2},{1,3},{2,0},{3,1},{4,6},{5,7},{6,4},{7,5},{8,10},{9,11},{10,... | collective-permute-start | bytes 393224 | tf_op jit(solution)/shard_map/ppermute | solution.py:18
  29.9 19.2 %collective-permute-start.1 = (bf16[2,128,256]{2,1,0:T(8,128)(2,1)S(1)}, bf16[2,128,256]{2,1,0:T(8,128)(2,1)S(1)}, u32[]{:S(2)}, u32[]{:S(2)}) collective-permute-start(bf16[2,128,256]{2,1,0:T(8,128)(2,1)S(1)} %get-tuple-element.22), channel_id=1, source_target_pairs={{0,1},{1,2},{2,3},{3,0},{4,5},{5,6},{6,7},{7,4},{8,9},{9,10},{10,1... | collective-permute-start | bytes 393224 | tf_op jit(solution)/shard_map/ppermute | solution.py:18
  30.9 18.2 %collective-permute-start.2 = (bf16[2,128,256]{2,1,0:T(8,128)(2,1)S(1)}, bf16[2,128,256]{2,1,0:T(8,128)(2,1)S(1)}, u32[]{:S(2)}, u32[]{:S(2)}) collective-permute-start(bf16[2,128,256]{2,1,0:T(8,128)(2,1)S(1)} %get-tuple-element.23), channel_id=1, source_target_pairs={{0,3},{1,0},{2,1},{3,2},{4,7},{5,4},{6,5},{7,6},{8,11},{9,8},{10,9... | collective-permute-start | bytes 393224 | tf_op jit(solution)/shard_map/ppermute | solution.py:18
  40.9 23.4 %copy-start = (bf16[1,2,256,256]{3,2,1,0:T(8,128)(2,1)S(1)}, bf16[1,2,256,256]{3,2,1,0:T(8,128)(2,1)}, u32[]{:S(2)}) copy-start(bf16[1,2,256,256]{3,2,1,0:T(8,128)(2,1)} %param.7) | copy-start | bytes 786436
  49.2 8.8 %collective-permute-start.4 = (bf16[2,128,256]{2,1,0:T(8,128)(2,1)S(1)}, bf16[2,128,256]{2,1,0:T(8,128)(2,1)S(1)}, u32[]{:S(2)}, u32[]{:S(2)}) collective-permute-start(bf16[2,128,256]{2,1,0:T(8,128)(2,1)S(1)} %add_convert_fusion.rest_0_), channel_id=1, source_target_pairs={{0,8},{4,12},{8,0},{12,4},{1,9},{5,13},{9,1},{13,5},{2,10},{6,14},... | collective-permute-start | bytes 393224 | tf_op jit(solution)/shard_map/ppermute | solution.py:18
  50.7 7.8 %collective-permute-start.8 = (bf16[1,128,256]{2,1,0:T(8,128)(2,1)S(1)}, bf16[1,128,256]{2,1,0:T(8,128)(2,1)S(1)}, u32[]{:S(2)}, u32[]{:S(2)}) collective-permute-start(bf16[1,128,256]{2,1,0:T(8,128)(2,1)S(1)} %get-tuple-element.29), channel_id=1, source_target_pairs={{0,3},{1,0},{2,1},{3,2},{4,7},{5,4},{6,5},{7,6},{8,11},{9,8},{10,9... | collective-permute-start | bytes 196616 | tf_op jit(solution)/shard_map/ppermute | solution.py:18
  54.1 8.0 %collective-permute-start.7 = (bf16[1,128,256]{2,1,0:T(8,128)(2,1)S(1)}, bf16[1,128,256]{2,1,0:T(8,128)(2,1)S(1)}, u32[]{:S(2)}, u32[]{:S(2)}) collective-permute-start(bf16[1,128,256]{2,1,0:T(8,128)(2,1)S(1)} %get-tuple-element.28), channel_id=1, source_target_pairs={{0,2},{1,3},{2,0},{3,1},{4,6},{5,7},{6,4},{7,5},{8,10},{9,11},{10,... | collective-permute-start | bytes 196616 | tf_op jit(solution)/shard_map/ppermute | solution.py:18
  55.9 6.2 %collective-permute-start.6 = (bf16[1,128,256]{2,1,0:T(8,128)(2,1)S(1)}, bf16[1,128,256]{2,1,0:T(8,128)(2,1)S(1)}, u32[]{:S(2)}, u32[]{:S(2)}) collective-permute-start(bf16[1,128,256]{2,1,0:T(8,128)(2,1)S(1)} %get-tuple-element.27), channel_id=1, source_target_pairs={{0,1},{1,2},{2,3},{3,0},{4,5},{5,6},{6,7},{7,4},{8,9},{9,10},{10,1... | collective-permute-start | bytes 196616 | tf_op jit(solution)/shard_map/ppermute | solution.py:18
  57.9 6.4 %collective-permute-start.12 = (bf16[2,128,256]{2,1,0:T(8,128)(2,1)S(1)}, bf16[2,128,256]{2,1,0:T(8,128)(2,1)S(1)}, u32[]{:S(2)}, u32[]{:S(2)}) collective-permute-start(bf16[2,128,256]{2,1,0:T(8,128)(2,1)S(1)} %add_convert_fusion.rest_0_), channel_id=1, source_target_pairs={{0,4},{4,0},{8,12},{12,8},{1,5},{5,1},{9,13},{13,9},{2,6},{6,2},{1... | collective-permute-start | bytes 393224 | tf_op jit(solution)/shard_map/ppermute | solution.py:359
  57.9 9.2 %collective-permute-start.5 = (bf16[2,128,256]{2,1,0:T(8,128)(2,1)S(1)}, bf16[2,128,256]{2,1,0:T(8,128)(2,1)S(1)}, u32[]{:S(2)}, u32[]{:S(2)}) collective-permute-start(bf16[2,128,256]{2,1,0:T(8,128)(2,1)S(1)} %collective-permute-done.4.rest_1_), channel_id=1, source_target_pairs={{0,4},{4,0},{8,12},{12,8},{1,5},{5,1},{9,13},{13,9},{2,6},{6,2},{1... | collective-permute-start | bytes 393224 | tf_op jit(solution)/shard_map/ppermute | solution.py:362
  62.2 5.0 %collective-permute-start.9 = (bf16[1,128,256]{2,1,0:T(8,128)(2,1)S(1)}, bf16[1,128,256]{2,1,0:T(8,128)(2,1)S(1)}, u32[]{:S(2)}, u32[]{:S(2)}) collective-permute-start(bf16[1,128,256]{2,1,0:T(8,128)(2,1)S(1)} %add_convert_fusion.1.rest_1_), channel_id=1, source_target_pairs={{0,8},{4,12},{8,0},{12,4},{1,9},{5,13},{9,1},{13,5},{2,10},{6,14},... | collective-permute-start | bytes 196616 | tf_op jit(solution)/shard_map/ppermute | solution.py:18
  62.8 4.4 %collective-permute-start.10 = (bf16[1,128,256]{2,1,0:T(8,128)(2,1)S(1)}, bf16[1,128,256]{2,1,0:T(8,128)(2,1)S(1)}, u32[]{:S(2)}, u32[]{:S(2)}) collective-permute-start(bf16[1,128,256]{2,1,0:T(8,128)(2,1)S(1)} %add_convert_fusion.1.rest_1_), channel_id=1, source_target_pairs={{0,4},{4,0},{8,12},{12,8},{1,5},{5,1},{9,13},{13,9},{2,6},{6,2},{1... | collective-permute-start | bytes 196616 | tf_op jit(solution)/shard_map/ppermute | solution.py:359
  62.8 4.4 %collective-permute-start.11 = (bf16[1,128,256]{2,1,0:T(8,128)(2,1)S(1)}, bf16[1,128,256]{2,1,0:T(8,128)(2,1)S(1)}, u32[]{:S(2)}, u32[]{:S(2)}) collective-permute-start(bf16[1,128,256]{2,1,0:T(8,128)(2,1)S(1)} %add_convert_fusion.1.rest_1_), channel_id=1, source_target_pairs={{12,0},{8,4},{4,8},{0,12},{13,1},{9,5},{5,9},{1,13},{14,2},{10,6},... | collective-permute-start | bytes 196616 | tf_op jit(solution)/shard_map/ppermute | solution.py:356
